TPU v7x, 512 devices: a whole 4x8x8 slice. The times are simulated.
512 devices in a mesh: wide: 64 (over y, x, core), narrow: 8 (over z).
Axes of the slice: x: 4, y: 8, z: 8, core: 2. Of those that a mesh axis runs over, the one named last changes fastest.
Arguments:
- effects_start: float32 [262144, 256], P(('wide', 'narrow')), may hold values from -3 to 3
- marginal: float32 [262144, 256], P(('wide', 'narrow')), may hold values from -6 to 6
- ld_diag: float32 [262144, 512], P(('wide', 'narrow')), may hold values from -1 to 1, as said below
- ld_upper: float32 [262144, 512], P(('wide', 'narrow')), may hold values from -1 to 1
- penalty_grid: float32 [16], replicated, may hold values from 0.1 to 1
- penalty_index: int32 [256], replicated, may hold values from 0 to 15
- dosages: bfloat16 [1024, 262144], P(None, ('wide', 'narrow')), may hold values from 0 to 2
- stack_weights: float32 [256, 256], replicated, may hold values from -0.375 to 0.375
Outputs:
- effects: float32 [262144, 256], P(('wide', 'narrow'))
- stacked: float32 [1024, 256], P(('wide', 'narrow'))
Inputs may be any that keep to these rules, and one draw needn't show every extreme that they name: `ld_diag`: each diagonal tile is symmetric.
All inputs are finite; a program needn't handle non-finite values.
Results may differ from a plain program's by a relative error of at most 0.0037.
Values sent between devices are 32-bit elements; how exact they have to be, the bound alone decides.
No kernel may reach another device: no remote copies, remote signals or barrier semaphores. Data moves between devices by JAX's collectives and lax.ppermute only.
A program may use at most 64 MiB of HBM per device.

v0:
```python
import math

import jax
import jax.numpy as jnp
from jax import lax
from jax.sharding import PartitionSpec as P

ITERS = 3


step_size = 0.5


def passed_along(block, axis, distance):
    devices = range(lax.axis_size(axis))
    route = [(i - distance, i) for i in devices if i - distance in devices]
    return lax.ppermute(block, axis, route)


def full_dot(left, right):
    return jnp.dot(left, right, precision=lax.Precision.HIGHEST, preferred_element_type=jnp.float32)


def transposed_dot(left, right):
    return lax.dot_general(
        left,
        right,
        (((0,), (0,)), ((), ())),
        precision=lax.Precision.HIGHEST,
        preferred_element_type=jnp.float32,
    )


def shards(
    effects_start, marginal, ld_diag, ld_upper, penalty_grid, penalty_index, dosages, stack_weights
):
    variants = ld_diag.shape[0]
    levels = penalty_grid.shape[0]
    picked = (penalty_index[None, :] == jnp.arange(levels, dtype=jnp.int32)[:, None]).astype(
        jnp.float32
    )
    threshold = step_size * jnp.sum(picked * penalty_grid[:, None], axis=0)
    effects = effects_start
    for sweep in range(ITERS):
        own_term = full_dot(ld_diag, effects)
        next_rows = passed_along(effects, ("wide", "narrow"), -1)
        handed = transposed_dot(ld_upper, effects)
        from_prev = passed_along(handed, ("wide", "narrow"), 1)
        coupled = full_dot(ld_upper, next_rows) + from_prev
        gradient = own_term + coupled - marginal
        moved = effects - step_size * gradient
        effects = jnp.sign(moved) * jnp.maximum(jnp.abs(moved) - threshold[None, :], 0.0)
    effects_low = effects.astype(jnp.bfloat16)
    wide_count = lax.axis_size("wide")
    narrow_count = lax.axis_size("narrow")
    shrink = 1.0 / math.sqrt(variants * wide_count * narrow_count)
    summed = lax.psum_scatter(
        jnp.dot(dosages, effects_low, preferred_element_type=jnp.float32),
        ("wide", "narrow"),
        scatter_dimension=0,
        tiled=True,
    )
    scores = summed * shrink
    stacked = full_dot(scores, stack_weights)
    return (effects, stacked)


def solution(mesh):
    return jax.shard_map(
        shards,
        mesh=mesh,
        in_specs=(
            P(("wide", "narrow"), None),
            P(("wide", "narrow"), None),
            P(("wide", "narrow"), None),
            P(("wide", "narrow"), None),
            P(),
            P(),
            P(None, ("wide", "narrow")),
            P(),
        ),
        out_specs=(P(("wide", "narrow"), None), P(("wide", "narrow"), None)),
        check_vma=False,
    )
```

profile of v0, /device:TPU:1, one launch (start us, length us, event | category | flops | bytes accessed | tf_op | source)
XLA Modules:
  0.0 368.7 jit_solution(9133103591232359373)
XLA Ops:
  7.2 0.0 copy-start
  7.2 0.0 copy-start.3
  7.2 0.0 copy-start.8
  7.2 0.0 copy-start.7
  7.2 0.0 copy-start.1
  7.2 0.0 all-reduce.3.cloned.1.call-start
  7.3 12.2 %collective-permute-start = (f32[512,256]{1,0:T(8,128)}, f32[512,256]{1,0:T(8,128)S(1)}, u32[]{:S(2)}, u32[]{:S(2)}) collective-permute-start(f32[512,256]{1,0:T(8,128)} %param.8), channel_id=1, source_target_pairs={{1,0},{2,1},{3,2},{4,3},{5,4},{6,5},{7,6},{8,7},{9,8},{10,9},{11,1... | collective-permute-start | bytes 1572872 | tf_op jit(solution)/shard_map/ppermute | solution.py:17
  19.5 0.0 copy-done
  19.5 2.9 fusion.20
  22.3 1.9 collective-permute-start.1
  24.2 0.0 copy-done.8
  24.3 0.0 copy-done.7
  24.3 0.1 select_reduce_fusion
  24.4 0.0 copy-done.3
  24.4 0.0 copy-done.1
  24.4 0.0 copy-start.2
  24.4 1.0 fusion.19
  25.4 14.2 %collective-permute-done.1 = f32[512,256]{1,0:T(8,128)S(1)} collective-permute-done((f32[512,256]{1,0:T(8,128)S(1)}, f32[512,256]{1,0:T(8,128)S(1)}, u32[]{:S(2)}, u32[]{:S(2)}) %collective-permute-start.1) | collective-permute-done | bytes 524320 | tf_op jit(solution)/shard_map/ppermute | solution.py:17
  39.6 0.0 collective-permute-done
  39.6 0.0 copy-done.2
  39.6 1.2 maximum_multiply_fusion.2
  40.8 1.8 convolution_bitcast_fusion.4
  42.7 1.9 collective-permute-start.3
  44.6 4.9 %collective-permute-start.2 = (f32[512,256]{1,0:T(8,128)S(1)}, f32[512,256]{1,0:T(8,128)S(1)}, u32[]{:S(2)}, u32[]{:S(2)}) collective-permute-start(f32[512,256]{1,0:T(8,128)S(1)} %maximum_multiply_fusion.2), channel_id=1, source_target_pairs={{1,0},{2,1},{3,2},{4,3},{5,4},{6,5},{7,6},{8,7},{9,8},{10,9},{11,1... | collective-permute-start | bytes 1572872 | tf_op jit(solution)/shard_map/ppermute | solution.py:17
  49.4 1.0 convolution_bitcast_fusion.6
  50.5 8.6 %collective-permute-done.3 = f32[512,256]{1,0:T(8,128)S(1)} collective-permute-done((f32[512,256]{1,0:T(8,128)S(1)}, f32[512,256]{1,0:T(8,128)S(1)}, u32[]{:S(2)}, u32[]{:S(2)}) %collective-permute-start.3) | collective-permute-done | bytes 524320 | tf_op jit(solution)/shard_map/ppermute | solution.py:17
  59.0 2.1 collective-permute-done.2
  61.2 1.2 maximum_multiply_fusion.1
  62.4 1.8 convolution_bitcast_fusion.1
  64.2 1.9 collective-permute-start.5
  66.2 5.8 %collective-permute-start.4 = (f32[512,256]{1,0:T(8,128)S(1)}, f32[512,256]{1,0:T(8,128)S(1)}, u32[]{:S(2)}, u32[]{:S(2)}) collective-permute-start(f32[512,256]{1,0:T(8,128)S(1)} %maximum_multiply_fusion.1), channel_id=1, source_target_pairs={{1,0},{2,1},{3,2},{4,3},{5,4},{6,5},{7,6},{8,7},{9,8},{10,9},{11,1... | collective-permute-start | bytes 1572872 | tf_op jit(solution)/shard_map/ppermute | solution.py:17
  72.0 1.0 convolution_bitcast_fusion.3
  73.0 0.0 copy-start.5
  73.0 9.0 %collective-permute-done.5 = f32[512,256]{1,0:T(8,128)S(1)} collective-permute-done((f32[512,256]{1,0:T(8,128)S(1)}, f32[512,256]{1,0:T(8,128)S(1)}, u32[]{:S(2)}, u32[]{:S(2)}) %collective-permute-start.5) | collective-permute-done | bytes 524320 | tf_op jit(solution)/shard_map/ppermute | solution.py:17
  82.0 1.5 collective-permute-done.4
  83.5 1.2 maximum_multiply_fusion
  84.7 0.0 copy-done.5
  84.8 0.0 copy-start.4
  84.8 1.5 convolution_bitcast_fusion
  86.3 0.0 copy-done.4
  86.3 0.0 copy-start.6
  86.3 0.0 all-reduce.3.cloned.1.call-update
  86.3 273.6 %all-reduce.3.cloned.1.call-done = f32[1024,256]{0,1:T(8,128)} async-done(((f32[1024,256]{0,1:T(8,128)}), f32[1024,256]{0,1:T(8,128)}) %all-reduce.3.cloned.1.call-update) | async-done | bytes 1048592
  359.9 0.0 copy-done.6
  359.9 1.9 fusion.15
  (1 shorter events, 0.0 us)
Async XLA Ops:
  7.2 12.3 %copy-start = (f32[512,512]{1,0:T(8,128)S(1)}, f32[512,512]{1,0:T(8,128)}, u32[]{:S(2)}) copy-start(f32[512,512]{1,0:T(8,128)} %param.11) | copy-start | bytes 3145732
  7.2 17.2 %copy-start.3 = (f32[512,256]{1,0:T(8,128)S(1)}, f32[512,256]{1,0:T(8,128)}, u32[]{:S(2)}) copy-start(f32[512,256]{1,0:T(8,128)} %param.8) | copy-start | bytes 1572868
  7.2 17.1 %copy-start.8 = (f32[16]{0:T(128)S(1)}, f32[16]{0:T(128)}, u32[]{:S(2)}) copy-start(f32[16]{0:T(128)} %param.12) | copy-start | bytes 196
  7.2 17.1 %copy-start.7 = (s32[256]{0:T(256)S(1)}, s32[256]{0:T(256)}, u32[]{:S(2)}) copy-start(s32[256]{0:T(256)} %param.13) | copy-start | bytes 3076
  7.2 17.2 %copy-start.1 = (f32[512,512]{1,0:T(8,128)S(1)}, f32[512,512]{1,0:T(8,128)}, u32[]{:S(2)}) copy-start(f32[512,512]{1,0:T(8,128)} %param.10) | copy-start | bytes 3145732
  7.2 352.7 %all-reduce.3.cloned.1.call-start = ((), (), s32[]{:S(2)}) async-start(), calls=%async_computation | async-start | bytes 2097152
  7.3 32.3 %collective-permute-start = (f32[512,256]{1,0:T(8,128)}, f32[512,256]{1,0:T(8,128)S(1)}, u32[]{:S(2)}, u32[]{:S(2)}) collective-permute-start(f32[512,256]{1,0:T(8,128)} %param.8), channel_id=1, source_target_pairs={{1,0},{2,1},{3,2},{4,3},{5,4},{6,5},{7,6},{8,7},{9,8},{10,9},{11,1... | collective-permute-start | bytes 1572872 | tf_op jit(solution)/shard_map/ppermute | solution.py:17
  22.3 17.3 %collective-permute-start.1 = (f32[512,256]{1,0:T(8,128)S(1)}, f32[512,256]{1,0:T(8,128)S(1)}, u32[]{:S(2)}, u32[]{:S(2)}) collective-permute-start(f32[512,256]{1,0:T(8,128)S(1)} %fusion.20), channel_id=1, source_target_pairs={{0,1},{1,2},{2,3},{3,4},{4,5},{5,6},{6,7},{7,8},{8,9},{9,10},{10,1... | collective-permute-start | bytes 1572872 | tf_op jit(solution)/shard_map/ppermute | solution.py:17
  24.4 15.2 %copy-start.2 = (f32[512,256]{1,0:T(8,128)S(1)}, f32[512,256]{1,0:T(8,128)}, u32[]{:S(2)}) copy-start(f32[512,256]{1,0:T(8,128)} %param.9) | copy-start | bytes 1572868
  42.7 16.4 %collective-permute-start.3 = (f32[512,256]{1,0:T(8,128)S(1)}, f32[512,256]{1,0:T(8,128)S(1)}, u32[]{:S(2)}, u32[]{:S(2)}) collective-permute-start(f32[512,256]{1,0:T(8,128)S(1)} %convolution_bitcast_fusion.4), channel_id=1, source_target_pairs={{0,1},{1,2},{2,3},{3,4},{4,5},{5,6},{6,7},{7,8},{8,9},{9,10},{10,1... | collective-permute-start | bytes 1572872 | tf_op jit(solution)/shard_map/ppermute | solution.py:17
  44.6 16.6 %collective-permute-start.2 = (f32[512,256]{1,0:T(8,128)S(1)}, f32[512,256]{1,0:T(8,128)S(1)}, u32[]{:S(2)}, u32[]{:S(2)}) collective-permute-start(f32[512,256]{1,0:T(8,128)S(1)} %maximum_multiply_fusion.2), channel_id=1, source_target_pairs={{1,0},{2,1},{3,2},{4,3},{5,4},{6,5},{7,6},{8,7},{9,8},{10,9},{11,1... | collective-permute-start | bytes 1572872 | tf_op jit(solution)/shard_map/ppermute | solution.py:17
  64.2 17.7 %collective-permute-start.5 = (f32[512,256]{1,0:T(8,128)S(1)}, f32[512,256]{1,0:T(8,128)S(1)}, u32[]{:S(2)}, u32[]{:S(2)}) collective-permute-start(f32[512,256]{1,0:T(8,128)S(1)} %convolution_bitcast_fusion.1), channel_id=1, source_target_pairs={{0,1},{1,2},{2,3},{3,4},{4,5},{5,6},{6,7},{7,8},{8,9},{9,10},{10,1... | collective-permute-start | bytes 1572872 | tf_op jit(solution)/shard_map/ppermute | solution.py:17
  66.2 17.3 %collective-permute-start.4 = (f32[512,256]{1,0:T(8,128)S(1)}, f32[512,256]{1,0:T(8,128)S(1)}, u32[]{:S(2)}, u32[]{:S(2)}) collective-permute-start(f32[512,256]{1,0:T(8,128)S(1)} %maximum_multiply_fusion.1), channel_id=1, source_target_pairs={{1,0},{2,1},{3,2},{4,3},{5,4},{6,5},{7,6},{8,7},{9,8},{10,9},{11,1... | collective-permute-start | bytes 1572872 | tf_op jit(solution)/shard_map/ppermute | solution.py:17
  73.0 11.8 %copy-start.5 = (bf16[1024,512]{1,0:T(8,128)(2,1)S(1)}, bf16[1024,512]{1,0:T(8,128)(2,1)}, u32[]{:S(2)}) copy-start(bf16[1024,512]{1,0:T(8,128)(2,1)} %param.14) | copy-start | bytes 3145732
  84.8 1.5 copy-start.4
  86.3 273.7 %copy-start.6 = (f32[256,256]{1,0:T(8,128)S(1)}, f32[256,256]{1,0:T(8,128)}, u32[]{:S(2)}) copy-start(f32[256,256]{1,0:T(8,128)} %param.15) | copy-start | bytes 786436
Sparse Core Ops, SparseCore 0:
  86.4 273.4 all-reduce.2
where the time goes:
time: 369 us
  waiting for transfers between devices  309 us (84%)
  starting transfers between devices  28.6 us (8%)
  matrix products  16.6 us (4%)
  between operations  14.3 us (4%)
    unnamed x2, waiting for transfers between devices  274 us
    ppermute x6, waiting for transfers between devices, passed_along(): return lax.ppermute(block, axis, route)  35.4 us
    ppermute x6, starting transfers between devices, passed_along(): return lax.ppermute(block, axis, route)  28.6 us
    dot_general x7, matrix products, full_dot(): jnp.dot(left, right, precision=lax.Precision.HIGHEST, preferred_element_t...  8.61 us
  transfers between devices with their start and end apart: 7, of which 6 were waited for; matrix products, arithmetic and copies ran while one was open for 2% of the time, Pallas kernels for 0%

commit v1 on v0

v1 whole, which is shorter than its diff:
```python
import math

import jax
import jax.numpy as jnp
from jax import lax
from jax.sharding import Mesh, PartitionSpec as P

ITERS = 3
SPLIT = (("y", 8), ("x", 4), ("c", 2), ("z", 8))
ALL = tuple(name for name, _ in SPLIT)
STAGES = (("y", "x", "z"),)
PREC = lax.Precision.HIGH

step_size = 0.5


def passed_along(block, distance):
    count = lax.axis_size(ALL)
    route = [(i - distance, i) for i in range(count) if 0 <= i - distance < count]
    return lax.ppermute(block, ALL, route)


def dot(left, right):
    return jnp.dot(left, right, precision=PREC, preferred_element_type=jnp.float32)


def transposed_dot(left, right):
    return lax.dot_general(
        left, right, (((0,), (0,)), ((), ())), precision=PREC, preferred_element_type=jnp.float32
    )


def exchange_sum(block, axes):
    count = lax.axis_size(axes)
    rows = block.shape[0] // count
    got = lax.all_to_all(block.reshape(count, rows, block.shape[1]), axes, 0, 0, tiled=True)
    return jnp.sum(got, axis=0)


def shards(
    effects_start, marginal, ld_diag, ld_upper, penalty_grid, penalty_index, dosages, stack_weights
):
    variants = ld_diag.shape[0]
    levels = penalty_grid.shape[0]
    individuals = dosages.shape[0]
    picked = (penalty_index[None, :] == jnp.arange(levels, dtype=jnp.int32)[:, None]).astype(
        jnp.float32
    )
    threshold = step_size * jnp.sum(picked * penalty_grid[:, None], axis=0)

    core = lax.axis_index("c")
    lines = lax.axis_size(("y", "x"))
    by_core = dosages.reshape(lines, 2, individuals // (2 * lines), variants)

    def half(which):
        part = lax.dynamic_index_in_dim(by_core, which, axis=1, keepdims=False)
        return part.reshape(individuals // 2, variants)

    dosages_mine, dosages_other = half(core), half(1 - core)

    effects = effects_start
    for sweep in range(ITERS):
        ahead = passed_along(effects, -1)
        behind = passed_along(transposed_dot(ld_upper, effects), 1)
        gradient = dot(ld_diag, effects) + dot(ld_upper, ahead) + behind - marginal
        moved = effects - step_size * gradient
        effects = jnp.sign(moved) * jnp.maximum(jnp.abs(moved) - threshold[None, :], 0.0)

    low = effects.astype(jnp.bfloat16)
    other = jnp.dot(dosages_other, low, preferred_element_type=jnp.float32)
    got = lax.ppermute(other, "c", [(0, 1), (1, 0)])
    summed = jnp.dot(dosages_mine, low, preferred_element_type=jnp.float32) + got
    for axes in STAGES:
        summed = exchange_sum(summed, axes)
    shrink = 1.0 / math.sqrt(variants * lax.axis_size(ALL))
    scores = summed * shrink
    stacked = jnp.dot(
        scores, stack_weights, precision=lax.Precision.HIGHEST, preferred_element_type=jnp.float32
    )
    return (effects, stacked)


def solution(mesh):
    fine = Mesh(mesh.devices.reshape([size for _, size in SPLIT]), ALL)
    return jax.shard_map(
        shards,
        mesh=fine,
        in_specs=(
            P(ALL, None),
            P(ALL, None),
            P(ALL, None),
            P(ALL, None),
            P(),
            P(),
            P(None, ALL),
            P(),
        ),
        out_specs=(P(ALL, None), P(ALL, None)),
        check_vma=False,
    )
```

time: 369 us -> 120 us (0.33)
  waiting for transfers between devices: 309 us -> 37.4 us
  blocking collectives: 0 us -> 36.5 us
  between operations: 14.3 us -> 0.87 us
  matrix products: 16.6 us -> 11.6 us
    unnamed x2 -> x0, waiting for transfers between devices: 274 us -> none
    all_to_all x0 -> x1, blocking collectives: none -> 36.5 us  [exchange_sum(): lax.all_to_all(block.reshape(count, rows, block.shape[1]), axes, 0, 0, ti...]
    dot_general x11 -> x12, matrix products: 16.6 us -> 11.6 us  [the longest x6 5.38 us: dot(): jnp.dot(left, right, precision=PREC, preferred_element_type=jnp.float32)]
    ppermute x6 -> x7, waiting for transfers between devices: 35.4 us -> 37.4 us  [the longest x6 35.6 us: passed_along(): return lax.ppermute(block, ALL, route)]
    ppermute x6 -> x7, starting transfers between devices: 28.6 us -> 30.3 us  [the longest x6 28.4 us: passed_along(): return lax.ppermute(block, ALL, route)]
  transfers between devices with their start and end apart: 7 -> 7, of which waited for: 6 -> 6; matrix products, arithmetic and copies ran while one was open for 2% -> 4% of each run, Pallas kernels for 0% -> 0%
where the time goes in v1:
time: 120 us; the launch traced here: 119 us
  waiting for transfers between devices  37.4 us (31%)
  blocking collectives  36.5 us (30%)
  starting transfers between devices  30.3 us (25%)
  matrix products  11.6 us (10%)
  local copies, waits for them, and re-layouts  2.3 us (2%)
    all_to_all x1, blocking collectives, exchange_sum(): lax.all_to_all(block.reshape(count, rows, block.shape[1]), axes, 0, 0, ti...  36.5 us
    ppermute x6, waiting for transfers between devices, passed_along(): return lax.ppermute(block, ALL, route)  35.6 us
    ppermute x6, starting transfers between devices, passed_along(): return lax.ppermute(block, ALL, route)  28.4 us
    dot_general x6, matrix products, dot(): jnp.dot(left, right, precision=PREC, preferred_element_type=jnp.float32)  5.38 us
    dot_general x3, matrix products, transposed_dot(): lax.dot_general(left, right, (((0,), (0,)), ((), ())), precision=PREC, pr...  4.84 us
  transfers between devices with their start and end apart: 7, of which 6 were waited for; matrix products, arithmetic and copies ran while one was open for 4% of the time, Pallas kernels for 0%

profile of v1, /device:TPU:1, one launch (start us, length us, event | category | flops | bytes accessed | tf_op | source)
XLA Modules:
  0.0 119.4 jit_solution(820965985768253708)
XLA Ops:
  0.6 0.0 copy-start
  0.6 0.0 copy-start.4
  0.7 0.0 copy-start.7
  0.7 0.0 copy-start.6
  0.7 0.0 copy-start.1
  0.7 12.2 %collective-permute-start = (f32[512,256]{1,0:T(8,128)}, f32[512,256]{1,0:T(8,128)S(1)}, u32[]{:S(2)}, u32[]{:S(2)}) collective-permute-start(f32[512,256]{1,0:T(8,128)} %param.8), channel_id=1, source_target_pairs={{1,0},{2,1},{3,2},{4,3},{5,4},{6,5},{7,6},{8,7},{9,8},{10,9},{11,1... | collective-permute-start | bytes 1572872 | tf_op jit(solution)/shard_map/ppermute | solution.py:20
  12.9 0.0 copy-done
  12.9 2.0 %fusion.22 = f32[512,256]{1,0:T(8,128)S(1)} fusion(f32[512,512]{1,0:T(8,128)S(1)} %copy-done, f32[512,256]{1,0:T(8,128)} %param.8), kind=kOutput, calls=%fused_computation.36 | convolution fusion | flops 402653184 | bytes 2097152 | tf_op jit(solution)/shard_map/dot_general | solution.py:28
  14.9 1.9 %collective-permute-start.1 = (f32[512,256]{1,0:T(8,128)S(1)}, f32[512,256]{1,0:T(8,128)S(1)}, u32[]{:S(2)}, u32[]{:S(2)}) collective-permute-start(f32[512,256]{1,0:T(8,128)S(1)} %fusion.22), channel_id=1, source_target_pairs={{0,1},{1,2},{2,3},{3,4},{4,5},{5,6},{6,7},{7,8},{8,9},{9,10},{10,1... | collective-permute-start | bytes 1572872 | tf_op jit(solution)/shard_map/ppermute | solution.py:20
  16.9 0.0 copy-done.7
  16.9 0.0 copy-done.6
  16.9 0.1 select_reduce_fusion
  17.0 0.0 copy-done.4
  17.0 0.0 copy-done.1
  17.0 0.0 copy-start.2
  17.0 0.6 fusion.21
  17.6 14.6 %collective-permute-done.1 = f32[512,256]{1,0:T(8,128)S(1)} collective-permute-done((f32[512,256]{1,0:T(8,128)S(1)}, f32[512,256]{1,0:T(8,128)S(1)}, u32[]{:S(2)}, u32[]{:S(2)}) %collective-permute-start.1) | collective-permute-done | bytes 524320 | tf_op jit(solution)/shard_map/ppermute | solution.py:20
  32.2 0.0 collective-permute-done
  32.2 0.0 copy-done.2
  32.2 0.8 maximum_multiply_fusion.2
  33.0 1.0 convolution_bitcast_fusion.1
  34.0 1.9 %collective-permute-start.3 = (f32[512,256]{1,0:T(8,128)S(1)}, f32[512,256]{1,0:T(8,128)S(1)}, u32[]{:S(2)}, u32[]{:S(2)}) collective-permute-start(f32[512,256]{1,0:T(8,128)S(1)} %convolution_bitcast_fusion.1), channel_id=1, source_target_pairs={{0,1},{1,2},{2,3},{3,4},{4,5},{5,6},{6,7},{7,8},{8,9},{9,10},{10,1... | collective-permute-start | bytes 1572872 | tf_op jit(solution)/shard_map/ppermute | solution.py:20
  36.0 4.9 %collective-permute-start.2 = (f32[512,256]{1,0:T(8,128)S(1)}, f32[512,256]{1,0:T(8,128)S(1)}, u32[]{:S(2)}, u32[]{:S(2)}) collective-permute-start(f32[512,256]{1,0:T(8,128)S(1)} %maximum_multiply_fusion.2), channel_id=1, source_target_pairs={{1,0},{2,1},{3,2},{4,3},{5,4},{6,5},{7,6},{8,7},{9,8},{10,9},{11,1... | collective-permute-start | bytes 1572872 | tf_op jit(solution)/shard_map/ppermute | solution.py:20
  40.8 0.6 fusion.23
  41.4 9.0 %collective-permute-done.3 = f32[512,256]{1,0:T(8,128)S(1)} collective-permute-done((f32[512,256]{1,0:T(8,128)S(1)}, f32[512,256]{1,0:T(8,128)S(1)}, u32[]{:S(2)}, u32[]{:S(2)}) %collective-permute-start.3) | collective-permute-done | bytes 524320 | tf_op jit(solution)/shard_map/ppermute | solution.py:20
  50.4 2.1 %collective-permute-done.2 = f32[512,256]{1,0:T(8,128)S(1)} collective-permute-done((f32[512,256]{1,0:T(8,128)S(1)}, f32[512,256]{1,0:T(8,128)S(1)}, u32[]{:S(2)}, u32[]{:S(2)}) %collective-permute-start.2) | collective-permute-done | bytes 524320 | tf_op jit(solution)/shard_map/ppermute | solution.py:20
  52.5 0.8 maximum_multiply_fusion.1
  53.4 1.8 %convolution_bitcast_fusion = f32[512,256]{1,0:T(8,128)} fusion(f32[512,256]{1,0:T(8,128)S(1)} %maximum_multiply_fusion.1, f32[512,512]{1,0:T(8,128)S(1)} %copy-done), kind=kOutput, calls=%fused_computation.8 | convolution fusion | flops 402653184 | bytes 2097152 | tf_op jit(solution)/shard_map/dot_general | solution.py:28
  55.1 1.9 %collective-permute-start.5 = (f32[512,256]{1,0:T(8,128)}, f32[512,256]{1,0:T(8,128)}, u32[]{:S(2)}, u32[]{:S(2)}) collective-permute-start(f32[512,256]{1,0:T(8,128)} %convolution_bitcast_fusion), channel_id=1, source_target_pairs={{0,1},{1,2},{2,3},{3,4},{4,5},{5,6},{6,7},{7,8},{8,9},{9,10},{10,1... | collective-permute-start | bytes 1572872 | tf_op jit(solution)/shard_map/ppermute | solution.py:20
  57.1 5.6 %collective-permute-start.4 = (f32[512,256]{1,0:T(8,128)S(1)}, f32[512,256]{1,0:T(8,128)}, u32[]{:S(2)}, u32[]{:S(2)}) collective-permute-start(f32[512,256]{1,0:T(8,128)S(1)} %maximum_multiply_fusion.1), channel_id=1, source_target_pairs={{1,0},{2,1},{3,2},{4,3},{5,4},{6,5},{7,6},{8,7},{9,8},{10,9},{11,1... | collective-permute-start | bytes 1572872 | tf_op jit(solution)/shard_map/ppermute | solution.py:20
  62.7 1.3 %constant_dynamic-slice_fusion.1 = (bf16[32,1,16,512]{3,2,1,0:T(8,128)(2,1)S(1)}, bf16[32,1,16,512]{3,2,1,0:T(8,128)(2,1)S(1)}) fusion(bf16[32,2,16,512]{3,2,1,0:T(8,128)(2,1)} %bitcast.54, s32[]{:T(128)S(6)} %select_n.7, s32[]{:T(128)S(6)} %select_n.8), kind=kLoop, calls=%fused_computation.32 | loop fusion | bytes 2097160 | tf_op jit(solution)/shard_map/jit(dynamic_index_in_dim)/dynamic_slice | solution.py:56
  64.0 0.6 fusion.24
  64.6 8.6 %collective-permute-done.5 = f32[512,256]{1,0:T(8,128)} collective-permute-done((f32[512,256]{1,0:T(8,128)}, f32[512,256]{1,0:T(8,128)}, u32[]{:S(2)}, u32[]{:S(2)}) %collective-permute-start.5) | collective-permute-done | bytes 524320 | tf_op jit(solution)/shard_map/ppermute | solution.py:20
  73.2 1.2 %collective-permute-done.4 = f32[512,256]{1,0:T(8,128)} collective-permute-done((f32[512,256]{1,0:T(8,128)S(1)}, f32[512,256]{1,0:T(8,128)}, u32[]{:S(2)}, u32[]{:S(2)}) %collective-permute-start.4) | collective-permute-done | bytes 524320 | tf_op jit(solution)/shard_map/ppermute | solution.py:20
  74.4 2.0 %maximum_multiply_fusion = f32[512,256]{1,0:T(8,128)S(1)} fusion(f32[512,256]{1,0:T(8,128)S(1)} %maximum_multiply_fusion.1, f32[512,256]{1,0:T(8,128)S(1)} %copy-done.2, f32[512,256]{1,0:T(8,128)} %collective-permute-done.5, f32[256,512]{0,1:T(8,128)S(1)} %fusion.24, f32[512,256]{1,0:T(8,128)} %collective-permute-done.4, f32[512,512]{1,0:T(8,128)S(1)} %copy-done, ...), kind=kOutput, calls=%fused_computation.20 | convolution fusion | flops 403963904 | bytes 4195328 | tf_op jit(solution)/shard_map/dot_general | solution.py:24
  76.4 0.0 copy-start.3
  76.4 0.3 fusion.14
  76.7 1.9 %collective-permute-start.6 = (f32[512,256]{1,0:T(8,128)S(1)}, f32[512,256]{1,0:T(8,128)S(1)}, u32[]{:S(2)}, u32[]{:S(2)}) collective-permute-start(f32[512,256]{1,0:T(8,128)S(1)} %fusion.14), channel_id=1, source_target_pairs={{0,8},{8,0},{1,9},{9,1},{2,10},{10,2},{3,11},{11,3},{4,12},{12,4},... | collective-permute-start | bytes 1572872 | tf_op jit(solution)/shard_map/ppermute | solution.py:71
  78.6 1.9 %collective-permute-done.6 = f32[512,256]{1,0:T(8,128)S(1)} collective-permute-done((f32[512,256]{1,0:T(8,128)S(1)}, f32[512,256]{1,0:T(8,128)S(1)}, u32[]{:S(2)}, u32[]{:S(2)}) %collective-permute-start.6) | collective-permute-done | bytes 524320 | tf_op jit(solution)/shard_map/ppermute | solution.py:71
  80.5 0.0 copy-done.3
  80.5 0.3 convolution_add_fusion.3
  80.8 0.3 reshape.26
  81.1 36.5 %all_to_all.5 = f32[256,2,256]{2,1,0:T(2,128)S(1)} all-to-all(f32[256,2,256]{2,1,0:T(2,128)S(1)} %reshape.26), channel_id=1, replica_groups=mesh['y'=8,'x'=4,'c'=2,'z'=8] {'y','x','z'}, dimensions={0} | all-to-all | bytes 1048576 | tf_op jit(solution)/shard_map/all_to_all | solution.py:36
  117.7 0.0 copy-start.5
  117.7 0.3 reduce_sum.19
  118.0 0.7 copy-done.5
  118.6 0.8 fusion.17
  (1 shorter events, 0.0 us)
Async XLA Ops:
  0.6 12.2 %copy-start = (f32[512,512]{1,0:T(8,128)S(1)}, f32[512,512]{1,0:T(8,128)}, u32[]{:S(2)}) copy-start(f32[512,512]{1,0:T(8,128)} %param.11) | copy-start | bytes 3145732
  0.6 16.3 %copy-start.4 = (f32[512,256]{1,0:T(8,128)S(1)}, f32[512,256]{1,0:T(8,128)}, u32[]{:S(2)}) copy-start(f32[512,256]{1,0:T(8,128)} %param.8) | copy-start | bytes 1572868
  0.7 16.2 %copy-start.7 = (f32[16]{0:T(128)S(1)}, f32[16]{0:T(128)}, u32[]{:S(2)}) copy-start(f32[16]{0:T(128)} %param.12) | copy-start | bytes 196
  0.7 16.2 %copy-start.6 = (s32[256]{0:T(256)S(1)}, s32[256]{0:T(256)}, u32[]{:S(2)}) copy-start(s32[256]{0:T(256)} %param.13) | copy-start | bytes 3076
  0.7 16.3 %copy-start.1 = (f32[512,512]{1,0:T(8,128)S(1)}, f32[512,512]{1,0:T(8,128)}, u32[]{:S(2)}) copy-start(f32[512,512]{1,0:T(8,128)} %param.10) | copy-start | bytes 3145732
  0.7 31.5 %collective-permute-start = (f32[512,256]{1,0:T(8,128)}, f32[512,256]{1,0:T(8,128)S(1)}, u32[]{:S(2)}, u32[]{:S(2)}) collective-permute-start(f32[512,256]{1,0:T(8,128)} %param.8), channel_id=1, source_target_pairs={{1,0},{2,1},{3,2},{4,3},{5,4},{6,5},{7,6},{8,7},{9,8},{10,9},{11,1... | collective-permute-start | bytes 1572872 | tf_op jit(solution)/shard_map/ppermute | solution.py:20
  14.9 17.3 %collective-permute-start.1 = (f32[512,256]{1,0:T(8,128)S(1)}, f32[512,256]{1,0:T(8,128)S(1)}, u32[]{:S(2)}, u32[]{:S(2)}) collective-permute-start(f32[512,256]{1,0:T(8,128)S(1)} %fusion.22), channel_id=1, source_target_pairs={{0,1},{1,2},{2,3},{3,4},{4,5},{5,6},{6,7},{7,8},{8,9},{9,10},{10,1... | collective-permute-start | bytes 1572872 | tf_op jit(solution)/shard_map/ppermute | solution.py:20
  17.0 15.2 %copy-start.2 = (f32[512,256]{1,0:T(8,128)S(1)}, f32[512,256]{1,0:T(8,128)}, u32[]{:S(2)}) copy-start(f32[512,256]{1,0:T(8,128)} %param.9) | copy-start | bytes 1572868
  34.0 16.4 %collective-permute-start.3 = (f32[512,256]{1,0:T(8,128)S(1)}, f32[512,256]{1,0:T(8,128)S(1)}, u32[]{:S(2)}, u32[]{:S(2)}) collective-permute-start(f32[512,256]{1,0:T(8,128)S(1)} %convolution_bitcast_fusion.1), channel_id=1, source_target_pairs={{0,1},{1,2},{2,3},{3,4},{4,5},{5,6},{6,7},{7,8},{8,9},{9,10},{10,1... | collective-permute-start | bytes 1572872 | tf_op jit(solution)/shard_map/ppermute | solution.py:20
  36.0 16.6 %collective-permute-start.2 = (f32[512,256]{1,0:T(8,128)S(1)}, f32[512,256]{1,0:T(8,128)S(1)}, u32[]{:S(2)}, u32[]{:S(2)}) collective-permute-start(f32[512,256]{1,0:T(8,128)S(1)} %maximum_multiply_fusion.2), channel_id=1, source_target_pairs={{1,0},{2,1},{3,2},{4,3},{5,4},{6,5},{7,6},{8,7},{9,8},{10,9},{11,1... | collective-permute-start | bytes 1572872 | tf_op jit(solution)/shard_map/ppermute | solution.py:20
  55.1 18.0 %collective-permute-start.5 = (f32[512,256]{1,0:T(8,128)}, f32[512,256]{1,0:T(8,128)}, u32[]{:S(2)}, u32[]{:S(2)}) collective-permute-start(f32[512,256]{1,0:T(8,128)} %convolution_bitcast_fusion), channel_id=1, source_target_pairs={{0,1},{1,2},{2,3},{3,4},{4,5},{5,6},{6,7},{7,8},{8,9},{9,10},{10,1... | collective-permute-start | bytes 1572872 | tf_op jit(solution)/shard_map/ppermute | solution.py:20
  57.1 17.3 %collective-permute-start.4 = (f32[512,256]{1,0:T(8,128)S(1)}, f32[512,256]{1,0:T(8,128)}, u32[]{:S(2)}, u32[]{:S(2)}) collective-permute-start(f32[512,256]{1,0:T(8,128)S(1)} %maximum_multiply_fusion.1), channel_id=1, source_target_pairs={{1,0},{2,1},{3,2},{4,3},{5,4},{6,5},{7,6},{8,7},{9,8},{10,9},{11,1... | collective-permute-start | bytes 1572872 | tf_op jit(solution)/shard_map/ppermute | solution.py:20
  76.4 4.1 %copy-start.3 = (f32[512,256]{1,0:T(8,128)}, f32[512,256]{1,0:T(8,128)S(1)}, u32[]{:S(2)}) copy-start(f32[512,256]{1,0:T(8,128)S(1)} %maximum_multiply_fusion) | copy-start | bytes 1572868
  76.7 3.8 %collective-permute-start.6 = (f32[512,256]{1,0:T(8,128)S(1)}, f32[512,256]{1,0:T(8,128)S(1)}, u32[]{:S(2)}, u32[]{:S(2)}) collective-permute-start(f32[512,256]{1,0:T(8,128)S(1)} %fusion.14), channel_id=1, source_target_pairs={{0,8},{8,0},{1,9},{9,1},{2,10},{10,2},{3,11},{11,3},{4,12},{12,4},... | collective-permute-start | bytes 1572872 | tf_op jit(solution)/shard_map/ppermute | solution.py:71
  117.7 1.0 copy-start.5

commit v2 on v1

--- a/solution.py
+++ b/solution.py
@@ -6,9 +6,9 @@
 from jax.sharding import Mesh, PartitionSpec as P
 
 ITERS = 3
-SPLIT = (("y", 8), ("x", 4), ("c", 2), ("z", 8))
+SPLIT = (("yh", 4), ("yl", 2), ("x", 4), ("c", 2), ("z", 8))
 ALL = tuple(name for name, _ in SPLIT)
-STAGES = (("y", "x", "z"),)
+STAGES = (("yl", "x"), ("yh", "z"))
 PREC = lax.Precision.HIGH
 
 step_size = 0.5
@@ -49,21 +49,24 @@
     threshold = step_size * jnp.sum(picked * penalty_grid[:, None], axis=0)
 
     core = lax.axis_index("c")
-    lines = lax.axis_size(("y", "x"))
-    by_core = dosages.reshape(lines, 2, individuals // (2 * lines), variants)
+    outer = [size for _, size in SPLIT[:4]]
+    by_core = dosages.reshape(*outer, individuals // math.prod(outer), variants)
 
     def half(which):
-        part = lax.dynamic_index_in_dim(by_core, which, axis=1, keepdims=False)
-        return part.reshape(individuals // 2, variants)
+        part = lax.dynamic_index_in_dim(by_core, which, axis=3, keepdims=False)
+        return part.transpose(1, 2, 0, 3, 4).reshape(individuals // 2, variants)
 
     dosages_mine, dosages_other = half(core), half(1 - core)
 
     effects = effects_start
-    for sweep in range(ITERS):
+    for _ in range(ITERS):
         ahead = passed_along(effects, -1)
-        behind = passed_along(transposed_dot(ld_upper, effects), 1)
-        gradient = dot(ld_diag, effects) + dot(ld_upper, ahead) + behind - marginal
-        moved = effects - step_size * gradient
+        handed = transposed_dot(ld_upper, effects)
+        behind = passed_along(handed, 1)
+        own = dot(ld_diag, effects)
+        known = own + dot(ld_upper, ahead) - marginal
+        known = lax.optimization_barrier(known)
+        moved = effects - step_size * (known + behind)
         effects = jnp.sign(moved) * jnp.maximum(jnp.abs(moved) - threshold[None, :], 0.0)
 
     low = effects.astype(jnp.bfloat16)
@@ -75,7 +78,7 @@
     shrink = 1.0 / math.sqrt(variants * lax.axis_size(ALL))
     scores = summed * shrink
     stacked = jnp.dot(
-        scores, stack_weights, precision=lax.Precision.HIGHEST, preferred_element_type=jnp.float32
+        scores, stack_weights, precision=PREC, preferred_element_type=jnp.float32
     )
     return (effects, stacked)
 

time: 120 us -> 112 us (0.933); the launches traced: 119 us -> 110 us
  starting transfers between devices: 30.3 us -> 26.6 us
  blocking collectives: 36.5 us -> 34.2 us
  waiting for transfers between devices: 37.4 us -> 35.7 us
  matrix products: 11.6 us -> 10.1 us
    ppermute x6, starting transfers between devices: 28.4 us -> 24.7 us  [passed_along(): return lax.ppermute(block, ALL, route)]
    all_to_all x1 -> x2, blocking collectives: 36.5 us -> 34.2 us  [exchange_sum(): lax.all_to_all(block.reshape(count, rows, block.shape[1]), axes, 0, 0, ti...]
    ppermute x6, waiting for transfers between devices: 35.6 us -> 33.8 us  [passed_along(): return lax.ppermute(block, ALL, route)]
  transfers between devices with their start and end apart: 7 -> 7, of which waited for: 6 -> 7; matrix products, arithmetic and copies ran while one was open for 4% -> 8% of each run, Pallas kernels for 0% -> 0%
where the time goes in v2:
time: 112 us; the launch traced here: 110 us
  waiting for transfers between devices  35.7 us (32%)
  blocking collectives  34.2 us (31%)
  starting transfers between devices  26.6 us (24%)
  matrix products  10.1 us (9%)
  local copies, waits for them, and re-layouts  1.93 us (2%)
    all_to_all x2, blocking collectives, exchange_sum(): lax.all_to_all(block.reshape(count, rows, block.shape[1]), axes, 0, 0, ti...  34.2 us
    ppermute x6, waiting for transfers between devices, passed_along(): return lax.ppermute(block, ALL, route)  33.8 us
    ppermute x6, starting transfers between devices, passed_along(): return lax.ppermute(block, ALL, route)  24.7 us
    dot_general x6, matrix products, dot(): jnp.dot(left, right, precision=PREC, preferred_element_type=jnp.float32)  4.61 us
    dot_general x3, matrix products, transposed_dot(): lax.dot_general(left, right, (((0,), (0,)), ((), ())), precision=PREC, pr...  4.08 us
  transfers between devices with their start and end apart: 7, of which 7 were waited for; matrix products, arithmetic and copies ran while one was open for 8% of the time, Pallas kernels for 0%

profile of v2, /device:TPU:1, one launch (start us, length us, event | category | flops | bytes accessed | tf_op | source)
XLA Modules:
  0.0 110.2 jit_solution(11183243614241419701)
XLA Ops:
  0.6 0.0 copy-start
  0.6 0.0 copy-start.5
  0.7 12.2 %collective-permute-start = (f32[512,256]{1,0:T(8,128)}, f32[512,256]{1,0:T(8,128)}, u32[]{:S(2)}, u32[]{:S(2)}) collective-permute-start(f32[512,256]{1,0:T(8,128)} %param.8), channel_id=1, source_target_pairs={{1,0},{2,1},{3,2},{4,3},{5,4},{6,5},{7,6},{8,7},{9,8},{10,9},{11,1... | collective-permute-start | bytes 1572872 | tf_op jit(solution)/shard_map/ppermute | solution.py:20
  12.8 0.0 copy-done
  12.9 2.1 %fusion.13 = f32[512,256]{1,0:T(8,128)S(1)} fusion(f32[512,512]{1,0:T(8,128)S(1)} %copy-done, f32[512,256]{1,0:T(8,128)} %param.8), kind=kOutput, calls=%fused_computation.27 | convolution fusion | flops 402653184 | bytes 2097152 | tf_op jit(solution)/shard_map/dot_general | solution.py:28
  14.9 1.9 %collective-permute-start.1 = (f32[512,256]{1,0:T(8,128)S(1)}, f32[512,256]{1,0:T(8,128)S(1)}, u32[]{:S(2)}, u32[]{:S(2)}) collective-permute-start(f32[512,256]{1,0:T(8,128)S(1)} %fusion.13), channel_id=1, source_target_pairs={{0,1},{1,2},{2,3},{3,4},{4,5},{5,6},{6,7},{7,8},{8,9},{9,10},{10,1... | collective-permute-start | bytes 1572872 | tf_op jit(solution)/shard_map/ppermute | solution.py:20
  16.9 0.0 copy-done.5
  16.9 0.0 copy-start.7
  16.9 0.0 copy-start.8
  16.9 0.0 copy-start.3
  16.9 0.1 constant_dynamic-slice_fusion.1
  17.0 0.5 copy-done.7
  17.6 0.0 copy-done.8
  17.6 0.0 copy-start.1
  17.6 0.1 select_reduce_fusion
  17.7 0.3 copy-done.3
  18.0 0.9 copy-done.1
  18.8 0.0 copy-start.4
  18.8 0.6 fusion.12
  19.4 5.4 %collective-permute-done = f32[512,256]{1,0:T(8,128)} collective-permute-done((f32[512,256]{1,0:T(8,128)}, f32[512,256]{1,0:T(8,128)}, u32[]{:S(2)}, u32[]{:S(2)}) %collective-permute-start) | collective-permute-done | bytes 524320 | tf_op jit(solution)/shard_map/ppermute | solution.py:20
  24.9 0.0 copy-done.4
  24.9 1.6 %fusion.2 = f32[512,256]{1,0:T(8,128)S(1)} fusion(f32[512,256]{1,0:T(8,128)S(1)} %copy-done.4, f32[512,256]{1,0:T(8,128)S(1)} %fusion.12, f32[512,512]{1,0:T(8,128)S(1)} %copy-done, f32[512,256]{1,0:T(8,128)} %collective-permute-done), kind=kOutput, calls=%fused_computation.5 | convolution fusion | flops 402915328 | bytes 3145728 | tf_op jit(solution)/shard_map/dot_general | solution.py:24
  26.5 5.7 %collective-permute-done.1 = f32[512,256]{1,0:T(8,128)S(1)} collective-permute-done((f32[512,256]{1,0:T(8,128)S(1)}, f32[512,256]{1,0:T(8,128)S(1)}, u32[]{:S(2)}, u32[]{:S(2)}) %collective-permute-start.1) | collective-permute-done | bytes 524320 | tf_op jit(solution)/shard_map/ppermute | solution.py:20
  32.2 0.2 maximum_multiply_fusion.2
  32.5 1.9 %collective-permute-start.2 = (f32[512,256]{1,0:T(8,128)S(1)}, f32[512,256]{1,0:T(8,128)S(1)}, u32[]{:S(2)}, u32[]{:S(2)}) collective-permute-start(f32[512,256]{1,0:T(8,128)S(1)} %maximum_multiply_fusion.2), channel_id=1, source_target_pairs={{1,0},{2,1},{3,2},{4,3},{5,4},{6,5},{7,6},{8,7},{9,8},{10,9},{11,1... | collective-permute-start | bytes 1572872 | tf_op jit(solution)/shard_map/ppermute | solution.py:20
  34.4 1.0 convolution_bitcast_fusion.1
  35.4 3.4 %collective-permute-start.3 = (f32[512,256]{1,0:T(8,128)S(1)}, f32[512,256]{1,0:T(8,128)S(1)}, u32[]{:S(2)}, u32[]{:S(2)}) collective-permute-start(f32[512,256]{1,0:T(8,128)S(1)} %convolution_bitcast_fusion.1), channel_id=1, source_target_pairs={{0,1},{1,2},{2,3},{3,4},{4,5},{5,6},{6,7},{7,8},{8,9},{9,10},{10,1... | collective-permute-start | bytes 1572872 | tf_op jit(solution)/shard_map/ppermute | solution.py:20
  38.8 0.6 fusion.14
  39.4 6.7 %collective-permute-done.2 = f32[512,256]{1,0:T(8,128)S(1)} collective-permute-done((f32[512,256]{1,0:T(8,128)S(1)}, f32[512,256]{1,0:T(8,128)S(1)}, u32[]{:S(2)}, u32[]{:S(2)}) %collective-permute-start.2) | collective-permute-done | bytes 524320 | tf_op jit(solution)/shard_map/ppermute | solution.py:20
  46.1 0.6 fusion.3
  46.7 5.1 %collective-permute-done.3 = f32[512,256]{1,0:T(8,128)S(1)} collective-permute-done((f32[512,256]{1,0:T(8,128)S(1)}, f32[512,256]{1,0:T(8,128)S(1)}, u32[]{:S(2)}, u32[]{:S(2)}) %collective-permute-start.3) | collective-permute-done | bytes 524320 | tf_op jit(solution)/shard_map/ppermute | solution.py:20
  51.8 0.2 maximum_multiply_fusion.1
  52.0 1.9 %collective-permute-start.4 = (f32[512,256]{1,0:T(8,128)S(1)}, f32[512,256]{1,0:T(8,128)S(1)}, u32[]{:S(2)}, u32[]{:S(2)}) collective-permute-start(f32[512,256]{1,0:T(8,128)S(1)} %maximum_multiply_fusion.1), channel_id=1, source_target_pairs={{1,0},{2,1},{3,2},{4,3},{5,4},{6,5},{7,6},{8,7},{9,8},{10,9},{11,1... | collective-permute-start | bytes 1572872 | tf_op jit(solution)/shard_map/ppermute | solution.py:20
  54.0 1.0 convolution_bitcast_fusion
  55.0 3.4 %collective-permute-start.5 = (f32[512,256]{1,0:T(8,128)S(1)}, f32[512,256]{1,0:T(8,128)S(1)}, u32[]{:S(2)}, u32[]{:S(2)}) collective-permute-start(f32[512,256]{1,0:T(8,128)S(1)} %convolution_bitcast_fusion), channel_id=1, source_target_pairs={{0,1},{1,2},{2,3},{3,4},{4,5},{5,6},{6,7},{7,8},{8,9},{9,10},{10,1... | collective-permute-start | bytes 1572872 | tf_op jit(solution)/shard_map/ppermute | solution.py:20
  58.3 0.6 fusion.15
  59.0 6.7 %collective-permute-done.4 = f32[512,256]{1,0:T(8,128)S(1)} collective-permute-done((f32[512,256]{1,0:T(8,128)S(1)}, f32[512,256]{1,0:T(8,128)S(1)}, u32[]{:S(2)}, u32[]{:S(2)}) %collective-permute-start.4) | collective-permute-done | bytes 524320 | tf_op jit(solution)/shard_map/ppermute | solution.py:20
  65.7 0.6 fusion.4
  66.3 4.2 %collective-permute-done.5 = f32[512,256]{1,0:T(8,128)S(1)} collective-permute-done((f32[512,256]{1,0:T(8,128)S(1)}, f32[512,256]{1,0:T(8,128)S(1)}, u32[]{:S(2)}, u32[]{:S(2)}) %collective-permute-start.5) | collective-permute-done | bytes 524320 | tf_op jit(solution)/shard_map/ppermute | solution.py:20
  70.5 0.2 maximum_multiply_fusion
  70.7 0.0 copy-start.2
  70.7 0.3 fusion.5
  71.0 1.9 %collective-permute-start.6 = (f32[512,256]{1,0:T(8,128)S(1)}, f32[512,256]{1,0:T(8,128)S(1)}, u32[]{:S(2)}, u32[]{:S(2)}) collective-permute-start(f32[512,256]{1,0:T(8,128)S(1)} %fusion.5), channel_id=1, source_target_pairs={{0,8},{8,0},{1,9},{9,1},{2,10},{10,2},{3,11},{11,3},{4,12},{12,4},... | collective-permute-start | bytes 1572872 | tf_op jit(solution)/shard_map/ppermute | solution.py:74
  73.0 1.8 %collective-permute-done.6 = f32[512,256]{1,0:T(8,128)S(1)} collective-permute-done((f32[512,256]{1,0:T(8,128)S(1)}, f32[512,256]{1,0:T(8,128)S(1)}, u32[]{:S(2)}, u32[]{:S(2)}) %collective-permute-start.6) | collective-permute-done | bytes 524320 | tf_op jit(solution)/shard_map/ppermute | solution.py:74
  74.8 0.0 copy-done.2
  74.8 0.3 convolution_add_fusion.3
  75.1 16.7 %all_to_all.10 = f32[8,64,256]{2,1,0:T(8,128)S(1)} all-to-all(f32[8,64,256]{2,1,0:T(8,128)S(1)} %bitcast.47), channel_id=1, replica_groups=mesh['yh'=4,'yl'=2,'x'=4,'c'=2,'z'=8] {'yl','x'}, dimensions={0} | all-to-all | bytes 1048576 | tf_op jit(solution)/shard_map/all_to_all | solution.py:36
  91.9 0.0 copy-start.6
  91.9 17.5 %all_to_all.11 = f32[32,2,256]{2,1,0:T(2,128)S(1)} all-to-all(f32[32,2,256]{2,1,0:T(2,128)S(1)} %reshape.28), channel_id=1, replica_groups=mesh['yh'=4,'yl'=2,'x'=4,'c'=2,'z'=8] {'yh','z'}, dimensions={0} | all-to-all | bytes 131072 | tf_op jit(solution)/shard_map/all_to_all | solution.py:36
  109.5 0.0 copy-done.6
  109.5 0.8 fusion.8
  (6 shorter events, 0.2 us)
Async XLA Ops:
  0.6 12.2 %copy-start = (f32[512,512]{1,0:T(8,128)S(1)}, f32[512,512]{1,0:T(8,128)}, u32[]{:S(2)}) copy-start(f32[512,512]{1,0:T(8,128)} %param.11) | copy-start | bytes 3145732
  0.6 16.2 %copy-start.5 = (bf16[1024,512]{1,0:T(8,128)(2,1)S(1)}, bf16[1024,512]{1,0:T(8,128)(2,1)}, u32[]{:S(2)}) copy-start(bf16[1024,512]{1,0:T(8,128)(2,1)} %param.14) | copy-start | bytes 3145732
  0.7 24.2 %collective-permute-start = (f32[512,256]{1,0:T(8,128)}, f32[512,256]{1,0:T(8,128)}, u32[]{:S(2)}, u32[]{:S(2)}) collective-permute-start(f32[512,256]{1,0:T(8,128)} %param.8), channel_id=1, source_target_pairs={{1,0},{2,1},{3,2},{4,3},{5,4},{6,5},{7,6},{8,7},{9,8},{10,9},{11,1... | collective-permute-start | bytes 1572872 | tf_op jit(solution)/shard_map/ppermute | solution.py:20
  14.9 17.3 %collective-permute-start.1 = (f32[512,256]{1,0:T(8,128)S(1)}, f32[512,256]{1,0:T(8,128)S(1)}, u32[]{:S(2)}, u32[]{:S(2)}) collective-permute-start(f32[512,256]{1,0:T(8,128)S(1)} %fusion.13), channel_id=1, source_target_pairs={{0,1},{1,2},{2,3},{3,4},{4,5},{5,6},{6,7},{7,8},{8,9},{9,10},{10,1... | collective-permute-start | bytes 1572872 | tf_op jit(solution)/shard_map/ppermute | solution.py:20
  16.9 0.7 copy-start.7
  16.9 0.7 copy-start.8
  16.9 1.1 copy-start.3
  17.6 1.3 %copy-start.1 = (f32[512,512]{1,0:T(8,128)S(1)}, f32[512,512]{1,0:T(8,128)}, u32[]{:S(2)}) copy-start(f32[512,512]{1,0:T(8,128)} %param.10) | copy-start | bytes 3145732
  18.8 6.0 %copy-start.4 = (f32[512,256]{1,0:T(8,128)S(1)}, f32[512,256]{1,0:T(8,128)}, u32[]{:S(2)}) copy-start(f32[512,256]{1,0:T(8,128)} %param.9) | copy-start | bytes 1572868
  32.5 13.7 %collective-permute-start.2 = (f32[512,256]{1,0:T(8,128)S(1)}, f32[512,256]{1,0:T(8,128)S(1)}, u32[]{:S(2)}, u32[]{:S(2)}) collective-permute-start(f32[512,256]{1,0:T(8,128)S(1)} %maximum_multiply_fusion.2), channel_id=1, source_target_pairs={{1,0},{2,1},{3,2},{4,3},{5,4},{6,5},{7,6},{8,7},{9,8},{10,9},{11,1... | collective-permute-start | bytes 1572872 | tf_op jit(solution)/shard_map/ppermute | solution.py:20
  35.4 16.4 %collective-permute-start.3 = (f32[512,256]{1,0:T(8,128)S(1)}, f32[512,256]{1,0:T(8,128)S(1)}, u32[]{:S(2)}, u32[]{:S(2)}) collective-permute-start(f32[512,256]{1,0:T(8,128)S(1)} %convolution_bitcast_fusion.1), channel_id=1, source_target_pairs={{0,1},{1,2},{2,3},{3,4},{4,5},{5,6},{6,7},{7,8},{8,9},{9,10},{10,1... | collective-permute-start | bytes 1572872 | tf_op jit(solution)/shard_map/ppermute | solution.py:20
  52.0 13.7 %collective-permute-start.4 = (f32[512,256]{1,0:T(8,128)S(1)}, f32[512,256]{1,0:T(8,128)S(1)}, u32[]{:S(2)}, u32[]{:S(2)}) collective-permute-start(f32[512,256]{1,0:T(8,128)S(1)} %maximum_multiply_fusion.1), channel_id=1, source_target_pairs={{1,0},{2,1},{3,2},{4,3},{5,4},{6,5},{7,6},{8,7},{9,8},{10,9},{11,1... | collective-permute-start | bytes 1572872 | tf_op jit(solution)/shard_map/ppermute | solution.py:20
  55.0 15.5 %collective-permute-start.5 = (f32[512,256]{1,0:T(8,128)S(1)}, f32[512,256]{1,0:T(8,128)S(1)}, u32[]{:S(2)}, u32[]{:S(2)}) collective-permute-start(f32[512,256]{1,0:T(8,128)S(1)} %convolution_bitcast_fusion), channel_id=1, source_target_pairs={{0,1},{1,2},{2,3},{3,4},{4,5},{5,6},{6,7},{7,8},{8,9},{9,10},{10,1... | collective-permute-start | bytes 1572872 | tf_op jit(solution)/shard_map/ppermute | solution.py:20
  70.7 4.1 %copy-start.2 = (f32[512,256]{1,0:T(8,128)}, f32[512,256]{1,0:T(8,128)S(1)}, u32[]{:S(2)}) copy-start(f32[512,256]{1,0:T(8,128)S(1)} %maximum_multiply_fusion) | copy-start | bytes 1572868
  71.0 3.8 %collective-permute-start.6 = (f32[512,256]{1,0:T(8,128)S(1)}, f32[512,256]{1,0:T(8,128)S(1)}, u32[]{:S(2)}, u32[]{:S(2)}) collective-permute-start(f32[512,256]{1,0:T(8,128)S(1)} %fusion.5), channel_id=1, source_target_pairs={{0,8},{8,0},{1,9},{9,1},{2,10},{10,2},{3,11},{11,3},{4,12},{12,4},... | collective-permute-start | bytes 1572872 | tf_op jit(solution)/shard_map/ppermute | solution.py:74
  91.9 17.6 %copy-start.6 = (f32[256,256]{1,0:T(8,128)S(1)}, f32[256,256]{1,0:T(8,128)}, u32[]{:S(2)}) copy-start(f32[256,256]{1,0:T(8,128)} %param.15) | copy-start | bytes 786436

commit v3 on v2

--- a/solution.py
+++ b/solution.py
@@ -3,6 +3,8 @@
 import jax
 import jax.numpy as jnp
 from jax import lax
+from jax.experimental import pallas as pl
+from jax.experimental.pallas import tpu as pltpu
 from jax.sharding import Mesh, PartitionSpec as P
 
 ITERS = 3
@@ -37,6 +39,41 @@
     return jnp.sum(got, axis=0)
 
 
+def turn_rows(rows_ref, mine_ref, other_ref, arrived):
+    core = lax.axis_index("c")
+    copies = []
+    for half, out_ref in enumerate((mine_ref, other_ref)):
+        which = lax.rem(core + half, 2)
+        for j in range(out_ref.shape[0]):
+            for k in range(out_ref.shape[1]):
+                copies.append(
+                    pltpu.make_async_copy(
+                        rows_ref.at[:, j, k, which], out_ref.at[j, k], arrived.at[len(copies)]
+                    )
+                )
+    for copy in copies:
+        copy.start()
+    for copy in copies:
+        copy.wait()
+
+
+def pick(by_core):
+    yh, yl, x, _, rows, variants = by_core.shape
+    half = jax.ShapeDtypeStruct((yl, x, yh, rows, variants), by_core.dtype)
+    return pl.pallas_call(
+        turn_rows,
+        in_specs=[pl.BlockSpec(memory_space=pltpu.HBM)],
+        out_specs=[pl.BlockSpec(memory_space=pltpu.VMEM)] * 2,
+        out_shape=[half, half],
+        scratch_shapes=[pltpu.SemaphoreType.DMA((2 * yl * x,))],
+        compiler_params=pltpu.CompilerParams(vmem_limit_bytes=4 * 1024 * 1024),
+        cost_estimate=pl.CostEstimate(
+            flops=0, bytes_accessed=4 * by_core.size, transcendentals=0
+        ),
+        name="pick",
+    )(by_core)
+
+
 def shards(
     effects_start, marginal, ld_diag, ld_upper, penalty_grid, penalty_index, dosages, stack_weights
 ):
@@ -48,15 +85,11 @@
     )
     threshold = step_size * jnp.sum(picked * penalty_grid[:, None], axis=0)
 
-    core = lax.axis_index("c")
     outer = [size for _, size in SPLIT[:4]]
     by_core = dosages.reshape(*outer, individuals // math.prod(outer), variants)
 
-    def half(which):
-        part = lax.dynamic_index_in_dim(by_core, which, axis=3, keepdims=False)
-        return part.transpose(1, 2, 0, 3, 4).reshape(individuals // 2, variants)
-
-    dosages_mine, dosages_other = half(core), half(1 - core)
+    halves = pick(by_core)
+    dosages_mine, dosages_other = [part.reshape(individuals // 2, variants) for part in halves]
 
     effects = effects_start
     for _ in range(ITERS):

time: 112 us -> 112 us (level)
  waiting for transfers between devices: 35.7 us -> 38.1 us
  local copies, waits for them, and re-layouts: 1.93 us -> 0.29 us
    ppermute x6, waiting for transfers between devices: 33.8 us -> 36.2 us  [passed_along(): return lax.ppermute(block, ALL, route)]
    unnamed x20 -> x18, local copies, waits for them, and re-layouts: 1.8 us -> 0.05 us
  transfers between devices with their start and end apart: 7 -> 7, of which waited for: 7 -> 7; matrix products, arithmetic and copies ran while one was open for 8% -> 7% of each run, Pallas kernels for 0% -> 0%
where the time goes in v3:
time: 112 us; the launch traced here: 111 us
  waiting for transfers between devices  38.1 us (34%)
  blocking collectives  34.2 us (31%)
  starting transfers between devices  26.7 us (24%)
  matrix products  9.13 us (8%)
    ppermute x6, waiting for transfers between devices, passed_along(): return lax.ppermute(block, ALL, route)  36.2 us
    all_to_all x2, blocking collectives, exchange_sum(): lax.all_to_all(block.reshape(count, rows, block.shape[1]), axes, 0, 0, ti...  34.2 us
    ppermute x6, starting transfers between devices, passed_along(): return lax.ppermute(block, ALL, route)  24.8 us
    dot_general x3, matrix products, transposed_dot(): lax.dot_general(left, right, (((0,), (0,)), ((), ())), precision=PREC, pr...  4.11 us
    dot_general x6, matrix products, dot(): jnp.dot(left, right, precision=PREC, preferred_element_type=jnp.float32)  3.57 us
  transfers between devices with their start and end apart: 7, of which 7 were waited for; matrix products, arithmetic and copies ran while one was open for 7% of the time, Pallas kernels for 0%

profile of v3, /device:TPU:1, one launch (start us, length us, event | category | flops | bytes accessed | tf_op | source)
XLA Modules:
  0.0 110.7 jit_solution(2877487520419094267)
XLA Ops:
  0.6 0.0 copy-start
  0.6 0.0 copy-start.7
  0.7 0.0 copy-start.8
  0.7 0.0 copy-start.1
  0.7 12.2 %collective-permute-start = (f32[512,256]{1,0:T(8,128)}, f32[512,256]{1,0:T(8,128)S(1)}, u32[]{:S(2)}, u32[]{:S(2)}) collective-permute-start(f32[512,256]{1,0:T(8,128)} %param.8), channel_id=1, source_target_pairs={{1,0},{2,1},{3,2},{4,3},{5,4},{6,5},{7,6},{8,7},{9,8},{10,9},{11,1... | collective-permute-start | bytes 1572872 | tf_op jit(solution)/shard_map/ppermute | solution.py:22
  12.9 0.0 copy-done
  12.9 0.0 copy-start.4
  12.9 2.1 %fusion.13 = f32[512,256]{1,0:T(8,128)S(1)} fusion(f32[512,512]{1,0:T(8,128)S(1)} %copy-done, f32[512,256]{1,0:T(8,128)} %param.8), kind=kOutput, calls=%fused_computation.26 | convolution fusion | flops 402653184 | bytes 2097152 | tf_op jit(solution)/shard_map/dot_general | solution.py:30
  15.0 0.0 copy-start.2
  15.0 2.1 %collective-permute-start.1 = (f32[512,256]{1,0:T(8,128)S(1)}, f32[512,256]{1,0:T(8,128)S(1)}, u32[]{:S(2)}, u32[]{:S(2)}) collective-permute-start(f32[512,256]{1,0:T(8,128)S(1)} %fusion.13), channel_id=1, source_target_pairs={{0,1},{1,2},{2,3},{3,4},{4,5},{5,6},{6,7},{7,8},{8,9},{9,10},{10,1... | collective-permute-start | bytes 1572872 | tf_op jit(solution)/shard_map/ppermute | solution.py:22
  17.1 0.0 copy-done.7
  17.1 0.0 copy-done.8
  17.1 0.1 select_reduce_fusion
  17.2 0.0 copy-done.1
  17.2 0.5 pick.1
  17.7 0.0 copy-done.4
  17.7 0.0 copy-done.2
  17.7 0.0 copy-start.5
  17.7 0.6 fusion.12
  18.3 6.6 %collective-permute-done = f32[512,256]{1,0:T(8,128)S(1)} collective-permute-done((f32[512,256]{1,0:T(8,128)}, f32[512,256]{1,0:T(8,128)S(1)}, u32[]{:S(2)}, u32[]{:S(2)}) %collective-permute-start) | collective-permute-done | bytes 524320 | tf_op jit(solution)/shard_map/ppermute | solution.py:22
  24.9 0.0 copy-done.5
  24.9 0.6 fusion.2
  25.5 6.9 %collective-permute-done.1 = f32[512,256]{1,0:T(8,128)S(1)} collective-permute-done((f32[512,256]{1,0:T(8,128)S(1)}, f32[512,256]{1,0:T(8,128)S(1)}, u32[]{:S(2)}, u32[]{:S(2)}) %collective-permute-start.1) | collective-permute-done | bytes 524320 | tf_op jit(solution)/shard_map/ppermute | solution.py:22
  32.4 0.2 maximum_multiply_fusion.2
  32.7 1.9 %collective-permute-start.2 = (f32[512,256]{1,0:T(8,128)S(1)}, f32[512,256]{1,0:T(8,128)S(1)}, u32[]{:S(2)}, u32[]{:S(2)}) collective-permute-start(f32[512,256]{1,0:T(8,128)S(1)} %maximum_multiply_fusion.2), channel_id=1, source_target_pairs={{1,0},{2,1},{3,2},{4,3},{5,4},{6,5},{7,6},{8,7},{9,8},{10,9},{11,1... | collective-permute-start | bytes 1572872 | tf_op jit(solution)/shard_map/ppermute | solution.py:22
  34.6 1.0 convolution_bitcast_fusion.3
  35.6 3.4 %collective-permute-start.3 = (f32[512,256]{1,0:T(8,128)S(1)}, f32[512,256]{1,0:T(8,128)S(1)}, u32[]{:S(2)}, u32[]{:S(2)}) collective-permute-start(f32[512,256]{1,0:T(8,128)S(1)} %convolution_bitcast_fusion.3), channel_id=1, source_target_pairs={{0,1},{1,2},{2,3},{3,4},{4,5},{5,6},{6,7},{7,8},{8,9},{9,10},{10,1... | collective-permute-start | bytes 1572872 | tf_op jit(solution)/shard_map/ppermute | solution.py:22
  39.0 0.6 fusion.14
  39.6 6.7 %collective-permute-done.2 = f32[512,256]{1,0:T(8,128)S(1)} collective-permute-done((f32[512,256]{1,0:T(8,128)S(1)}, f32[512,256]{1,0:T(8,128)S(1)}, u32[]{:S(2)}, u32[]{:S(2)}) %collective-permute-start.2) | collective-permute-done | bytes 524320 | tf_op jit(solution)/shard_map/ppermute | solution.py:22
  46.3 0.6 fusion.3
  46.9 5.1 %collective-permute-done.3 = f32[512,256]{1,0:T(8,128)S(1)} collective-permute-done((f32[512,256]{1,0:T(8,128)S(1)}, f32[512,256]{1,0:T(8,128)S(1)}, u32[]{:S(2)}, u32[]{:S(2)}) %collective-permute-start.3) | collective-permute-done | bytes 524320 | tf_op jit(solution)/shard_map/ppermute | solution.py:22
  52.0 0.2 maximum_multiply_fusion.1
  52.2 1.9 %collective-permute-start.4 = (f32[512,256]{1,0:T(8,128)S(1)}, f32[512,256]{1,0:T(8,128)S(1)}, u32[]{:S(2)}, u32[]{:S(2)}) collective-permute-start(f32[512,256]{1,0:T(8,128)S(1)} %maximum_multiply_fusion.1), channel_id=1, source_target_pairs={{1,0},{2,1},{3,2},{4,3},{5,4},{6,5},{7,6},{8,7},{9,8},{10,9},{11,1... | collective-permute-start | bytes 1572872 | tf_op jit(solution)/shard_map/ppermute | solution.py:22
  54.2 1.0 convolution_bitcast_fusion.2
  55.2 3.4 %collective-permute-start.5 = (f32[512,256]{1,0:T(8,128)S(1)}, f32[512,256]{1,0:T(8,128)S(1)}, u32[]{:S(2)}, u32[]{:S(2)}) collective-permute-start(f32[512,256]{1,0:T(8,128)S(1)} %convolution_bitcast_fusion.2), channel_id=1, source_target_pairs={{0,1},{1,2},{2,3},{3,4},{4,5},{5,6},{6,7},{7,8},{8,9},{9,10},{10,1... | collective-permute-start | bytes 1572872 | tf_op jit(solution)/shard_map/ppermute | solution.py:22
  58.5 0.6 fusion.15
  59.1 6.7 %collective-permute-done.4 = f32[512,256]{1,0:T(8,128)S(1)} collective-permute-done((f32[512,256]{1,0:T(8,128)S(1)}, f32[512,256]{1,0:T(8,128)S(1)}, u32[]{:S(2)}, u32[]{:S(2)}) %collective-permute-start.4) | collective-permute-done | bytes 524320 | tf_op jit(solution)/shard_map/ppermute | solution.py:22
  65.9 0.6 fusion.4
  66.5 4.2 %collective-permute-done.5 = f32[512,256]{1,0:T(8,128)S(1)} collective-permute-done((f32[512,256]{1,0:T(8,128)S(1)}, f32[512,256]{1,0:T(8,128)S(1)}, u32[]{:S(2)}, u32[]{:S(2)}) %collective-permute-start.5) | collective-permute-done | bytes 524320 | tf_op jit(solution)/shard_map/ppermute | solution.py:22
  70.7 0.2 maximum_multiply_fusion
  70.9 0.0 copy-start.3
  70.9 0.3 convolution_bitcast_fusion
  71.3 1.9 %collective-permute-start.6 = (f32[512,256]{0,1:T(8,128)S(1)}, f32[512,256]{0,1:T(8,128)S(1)}, u32[]{:S(2)}, u32[]{:S(2)}) collective-permute-start(f32[512,256]{0,1:T(8,128)S(1)} %convolution_bitcast_fusion), channel_id=1, source_target_pairs={{0,8},{8,0},{1,9},{9,1},{2,10},{10,2},{3,11},{11,3},{4,12},{12,4},... | collective-permute-start | bytes 1572872 | tf_op jit(solution)/shard_map/ppermute | solution.py:107
  73.2 1.9 %collective-permute-done.6 = f32[512,256]{0,1:T(8,128)S(1)} collective-permute-done((f32[512,256]{0,1:T(8,128)S(1)}, f32[512,256]{0,1:T(8,128)S(1)}, u32[]{:S(2)}, u32[]{:S(2)}) %collective-permute-start.6) | collective-permute-done | bytes 524320 | tf_op jit(solution)/shard_map/ppermute | solution.py:107
  75.1 0.0 copy-done.3
  75.1 0.4 fusion.5
  75.4 0.2 copy.36
  75.6 16.7 %all_to_all.10 = f32[8,64,256]{2,1,0:T(8,128)S(1)} all-to-all(f32[8,64,256]{2,1,0:T(8,128)S(1)} %bitcast.46), channel_id=1, replica_groups=mesh['yh'=4,'yl'=2,'x'=4,'c'=2,'z'=8] {'yl','x'}, dimensions={0} | all-to-all | bytes 1048576 | tf_op jit(solution)/shard_map/all_to_all | solution.py:38
  92.4 0.0 copy-start.6
  92.4 17.5 %all_to_all.11 = f32[32,2,256]{2,1,0:T(2,128)S(1)} all-to-all(f32[32,2,256]{2,1,0:T(2,128)S(1)} %reshape.28), channel_id=1, replica_groups=mesh['yh'=4,'yl'=2,'x'=4,'c'=2,'z'=8] {'yh','z'}, dimensions={0} | all-to-all | bytes 131072 | tf_op jit(solution)/shard_map/all_to_all | solution.py:38
  110.0 0.0 copy-done.6
  110.0 0.8 fusion.8
  (4 shorter events, 0.1 us)
Async XLA Ops:
  0.6 12.2 %copy-start = (f32[512,512]{1,0:T(8,128)S(1)}, f32[512,512]{1,0:T(8,128)}, u32[]{:S(2)}) copy-start(f32[512,512]{1,0:T(8,128)} %param.11) | copy-start | bytes 3145732
  0.6 16.4 %copy-start.7 = (s32[256]{0:T(256)S(1)}, s32[256]{0:T(256)}, u32[]{:S(2)}) copy-start(s32[256]{0:T(256)} %param.13) | copy-start | bytes 3076
  0.7 16.4 %copy-start.8 = (f32[16]{0:T(128)S(1)}, f32[16]{0:T(128)}, u32[]{:S(2)}) copy-start(f32[16]{0:T(128)} %param.12) | copy-start | bytes 196
  0.7 16.5 %copy-start.1 = (bf16[1024,512]{1,0:T(8,128)(2,1)S(1)}, bf16[1024,512]{1,0:T(8,128)(2,1)}, u32[]{:S(2)}) copy-start(bf16[1024,512]{1,0:T(8,128)(2,1)} %param.14) | copy-start | bytes 3145732
  0.7 24.2 %collective-permute-start = (f32[512,256]{1,0:T(8,128)}, f32[512,256]{1,0:T(8,128)S(1)}, u32[]{:S(2)}, u32[]{:S(2)}) collective-permute-start(f32[512,256]{1,0:T(8,128)} %param.8), channel_id=1, source_target_pairs={{1,0},{2,1},{3,2},{4,3},{5,4},{6,5},{7,6},{8,7},{9,8},{10,9},{11,1... | collective-permute-start | bytes 1572872 | tf_op jit(solution)/shard_map/ppermute | solution.py:22
  12.9 4.8 %copy-start.4 = (f32[512,256]{1,0:T(8,128)S(1)}, f32[512,256]{1,0:T(8,128)}, u32[]{:S(2)}) copy-start(f32[512,256]{1,0:T(8,128)} %param.8) | copy-start | bytes 1572868
  15.0 2.7 %copy-start.2 = (f32[512,512]{1,0:T(8,128)S(1)}, f32[512,512]{1,0:T(8,128)}, u32[]{:S(2)}) copy-start(f32[512,512]{1,0:T(8,128)} %param.10) | copy-start | bytes 3145732
  15.0 17.4 %collective-permute-start.1 = (f32[512,256]{1,0:T(8,128)S(1)}, f32[512,256]{1,0:T(8,128)S(1)}, u32[]{:S(2)}, u32[]{:S(2)}) collective-permute-start(f32[512,256]{1,0:T(8,128)S(1)} %fusion.13), channel_id=1, source_target_pairs={{0,1},{1,2},{2,3},{3,4},{4,5},{5,6},{6,7},{7,8},{8,9},{9,10},{10,1... | collective-permute-start | bytes 1572872 | tf_op jit(solution)/shard_map/ppermute | solution.py:22
  17.7 7.2 %copy-start.5 = (f32[512,256]{1,0:T(8,128)S(1)}, f32[512,256]{1,0:T(8,128)}, u32[]{:S(2)}) copy-start(f32[512,256]{1,0:T(8,128)} %param.9) | copy-start | bytes 1572868
  32.7 13.7 %collective-permute-start.2 = (f32[512,256]{1,0:T(8,128)S(1)}, f32[512,256]{1,0:T(8,128)S(1)}, u32[]{:S(2)}, u32[]{:S(2)}) collective-permute-start(f32[512,256]{1,0:T(8,128)S(1)} %maximum_multiply_fusion.2), channel_id=1, source_target_pairs={{1,0},{2,1},{3,2},{4,3},{5,4},{6,5},{7,6},{8,7},{9,8},{10,9},{11,1... | collective-permute-start | bytes 1572872 | tf_op jit(solution)/shard_map/ppermute | solution.py:22
  35.6 16.4 %collective-permute-start.3 = (f32[512,256]{1,0:T(8,128)S(1)}, f32[512,256]{1,0:T(8,128)S(1)}, u32[]{:S(2)}, u32[]{:S(2)}) collective-permute-start(f32[512,256]{1,0:T(8,128)S(1)} %convolution_bitcast_fusion.3), channel_id=1, source_target_pairs={{0,1},{1,2},{2,3},{3,4},{4,5},{5,6},{6,7},{7,8},{8,9},{9,10},{10,1... | collective-permute-start | bytes 1572872 | tf_op jit(solution)/shard_map/ppermute | solution.py:22
  52.2 13.7 %collective-permute-start.4 = (f32[512,256]{1,0:T(8,128)S(1)}, f32[512,256]{1,0:T(8,128)S(1)}, u32[]{:S(2)}, u32[]{:S(2)}) collective-permute-start(f32[512,256]{1,0:T(8,128)S(1)} %maximum_multiply_fusion.1), channel_id=1, source_target_pairs={{1,0},{2,1},{3,2},{4,3},{5,4},{6,5},{7,6},{8,7},{9,8},{10,9},{11,1... | collective-permute-start | bytes 1572872 | tf_op jit(solution)/shard_map/ppermute | solution.py:22
  55.2 15.5 %collective-permute-start.5 = (f32[512,256]{1,0:T(8,128)S(1)}, f32[512,256]{1,0:T(8,128)S(1)}, u32[]{:S(2)}, u32[]{:S(2)}) collective-permute-start(f32[512,256]{1,0:T(8,128)S(1)} %convolution_bitcast_fusion.2), channel_id=1, source_target_pairs={{0,1},{1,2},{2,3},{3,4},{4,5},{5,6},{6,7},{7,8},{8,9},{9,10},{10,1... | collective-permute-start | bytes 1572872 | tf_op jit(solution)/shard_map/ppermute | solution.py:22
  70.9 4.2 %copy-start.3 = (f32[512,256]{1,0:T(8,128)}, f32[512,256]{1,0:T(8,128)S(1)}, u32[]{:S(2)}) copy-start(f32[512,256]{1,0:T(8,128)S(1)} %maximum_multiply_fusion) | copy-start | bytes 1572868
  71.3 3.8 %collective-permute-start.6 = (f32[512,256]{0,1:T(8,128)S(1)}, f32[512,256]{0,1:T(8,128)S(1)}, u32[]{:S(2)}, u32[]{:S(2)}) collective-permute-start(f32[512,256]{0,1:T(8,128)S(1)} %convolution_bitcast_fusion), channel_id=1, source_target_pairs={{0,8},{8,0},{1,9},{9,1},{2,10},{10,2},{3,11},{11,3},{4,12},{12,4},... | collective-permute-start | bytes 1572872 | tf_op jit(solution)/shard_map/ppermute | solution.py:107
  92.4 17.6 %copy-start.6 = (f32[256,256]{1,0:T(8,128)S(1)}, f32[256,256]{1,0:T(8,128)}, u32[]{:S(2)}) copy-start(f32[256,256]{1,0:T(8,128)} %param.15) | copy-start | bytes 786436

commit v4 on v3

--- a/solution.py
+++ b/solution.py
@@ -57,6 +57,25 @@
         copy.wait()
 
 
+def bring_block(block_ref, out_ref, arrived):
+    copy = pltpu.make_async_copy(block_ref, out_ref, arrived)
+    copy.start()
+    copy.wait()
+
+
+def bring(block):
+    return pl.pallas_call(
+        bring_block,
+        in_specs=[pl.BlockSpec(memory_space=pltpu.HBM)],
+        out_specs=pl.BlockSpec(memory_space=pltpu.VMEM),
+        out_shape=jax.ShapeDtypeStruct(block.shape, block.dtype),
+        scratch_shapes=[pltpu.SemaphoreType.DMA],
+        compiler_params=pltpu.CompilerParams(vmem_limit_bytes=4 * 1024 * 1024),
+        cost_estimate=pl.CostEstimate(flops=0, bytes_accessed=8 * block.size, transcendentals=0),
+        name="bring",
+    )(block)
+
+
 def pick(by_core):
     yh, yl, x, _, rows, variants = by_core.shape
     half = jax.ShapeDtypeStruct((yl, x, yh, rows, variants), by_core.dtype)
@@ -91,6 +110,7 @@
     halves = pick(by_core)
     dosages_mine, dosages_other = [part.reshape(individuals // 2, variants) for part in halves]
 
+    stack_weights = bring(stack_weights)
     effects = effects_start
     for _ in range(ITERS):
         ahead = passed_along(effects, -1)
@@ -106,13 +126,9 @@
     other = jnp.dot(dosages_other, low, preferred_element_type=jnp.float32)
     got = lax.ppermute(other, "c", [(0, 1), (1, 0)])
     summed = jnp.dot(dosages_mine, low, preferred_element_type=jnp.float32) + got
-    for axes in STAGES:
-        summed = exchange_sum(summed, axes)
     shrink = 1.0 / math.sqrt(variants * lax.axis_size(ALL))
-    scores = summed * shrink
-    stacked = jnp.dot(
-        scores, stack_weights, precision=PREC, preferred_element_type=jnp.float32
-    )
+    scores = exchange_sum(summed, STAGES[0]) * shrink
+    stacked = exchange_sum(dot(scores, stack_weights), STAGES[1])
     return (effects, stacked)
 
 

time: 112 us -> 113 us (level)
  blocking collectives: 34.2 us -> 17.4 us
  starting transfers between devices: 26.7 us -> 34.9 us
  waiting for transfers between devices: 38.1 us -> 46.2 us
    all_to_all x2 -> x1, blocking collectives: 34.2 us -> 17.4 us  [exchange_sum(): lax.all_to_all(block.reshape(count, rows, block.shape[1]), axes, 0, 0, ti...]
    all_to_all x0 -> x1, starting transfers between devices: none -> 8.2 us  [exchange_sum(): lax.all_to_all(block.reshape(count, rows, block.shape[1]), axes, 0, 0, ti...]
    all_to_all x0 -> x1, waiting for transfers between devices: none -> 8.17 us  [exchange_sum(): lax.all_to_all(block.reshape(count, rows, block.shape[1]), axes, 0, 0, ti...]
    dot_general x6 -> x7, matrix products: 3.57 us -> 3.78 us  [dot(): jnp.dot(left, right, precision=PREC, preferred_element_type=jnp.float32)]
  transfers between devices with their start and end apart: 7 -> 8, of which waited for: 7 -> 8; matrix products, arithmetic and copies ran while one was open for 7% -> 7% of each run, Pallas kernels for 0% -> 0%
where the time goes in v4:
time: 113 us; the launch traced here: 111 us
  waiting for transfers between devices  46.2 us (41%)
  starting transfers between devices  34.9 us (31%)
  blocking collectives  17.4 us (15%)
  matrix products  8.58 us (8%)
  other arithmetic  1.48 us (1%)
    ppermute x6, waiting for transfers between devices, passed_along(): return lax.ppermute(block, ALL, route)  36.2 us
    ppermute x6, starting transfers between devices, passed_along(): return lax.ppermute(block, ALL, route)  24.8 us
    all_to_all x1, blocking collectives, exchange_sum(): lax.all_to_all(block.reshape(count, rows, block.shape[1]), axes, 0, 0, ti...  17.4 us
    all_to_all x1, starting transfers between devices, exchange_sum(): lax.all_to_all(block.reshape(count, rows, block.shape[1]), axes, 0, 0, ti...  8.2 us
    all_to_all x1, waiting for transfers between devices, exchange_sum(): lax.all_to_all(block.reshape(count, rows, block.shape[1]), axes, 0, 0, ti...  8.17 us
    dot_general x3, matrix products, transposed_dot(): lax.dot_general(left, right, (((0,), (0,)), ((), ())), precision=PREC, pr...  4.11 us
    dot_general x7, matrix products, dot(): jnp.dot(left, right, precision=PREC, preferred_element_type=jnp.float32)  3.78 us
  transfers between devices with their start and end apart: 8, of which 8 were waited for; matrix products, arithmetic and copies ran while one was open for 7% of the time, Pallas kernels for 0%

profile of v4, /device:TPU:1, one launch (start us, length us, event | category | flops | bytes accessed | tf_op | source)
XLA Modules:
  0.0 111.1 jit_solution(15502292820544316911)
XLA Ops:
  0.6 0.0 copy-start
  0.6 0.0 copy-start.8
  0.7 0.0 copy-start.7
  0.7 0.0 copy-start.1
  0.7 12.2 %collective-permute-start = (f32[512,256]{1,0:T(8,128)}, f32[512,256]{1,0:T(8,128)S(1)}, u32[]{:S(2)}, u32[]{:S(2)}) collective-permute-start(f32[512,256]{1,0:T(8,128)} %param.8), channel_id=1, source_target_pairs={{1,0},{2,1},{3,2},{4,3},{5,4},{6,5},{7,6},{8,7},{9,8},{10,9},{11,1... | collective-permute-start | bytes 1572872 | tf_op jit(solution)/shard_map/ppermute | solution.py:22
  12.9 0.0 copy-done
  12.9 0.0 copy-start.5
  12.9 2.1 %fusion.13 = f32[512,256]{1,0:T(8,128)S(1)} fusion(f32[512,512]{1,0:T(8,128)S(1)} %copy-done, f32[512,256]{1,0:T(8,128)} %param.8), kind=kOutput, calls=%fused_computation.26 | convolution fusion | flops 402653184 | bytes 2097152 | tf_op jit(solution)/shard_map/dot_general | solution.py:30
  15.0 0.0 copy-start.3
  15.0 2.1 %collective-permute-start.1 = (f32[512,256]{1,0:T(8,128)S(1)}, f32[512,256]{1,0:T(8,128)S(1)}, u32[]{:S(2)}, u32[]{:S(2)}) collective-permute-start(f32[512,256]{1,0:T(8,128)S(1)} %fusion.13), channel_id=1, source_target_pairs={{0,1},{1,2},{2,3},{3,4},{4,5},{5,6},{6,7},{7,8},{8,9},{9,10},{10,1... | collective-permute-start | bytes 1572872 | tf_op jit(solution)/shard_map/ppermute | solution.py:22
  17.1 0.0 copy-done.8
  17.1 0.0 copy-done.7
  17.1 0.1 select_reduce_fusion
  17.2 0.0 copy-done.1
  17.2 0.5 pick.1
  17.7 0.0 copy-done.5
  17.7 0.0 copy-done.3
  17.7 0.0 copy-start.6
  17.7 0.6 fusion.12
  18.3 6.6 %collective-permute-done = f32[512,256]{1,0:T(8,128)S(1)} collective-permute-done((f32[512,256]{1,0:T(8,128)}, f32[512,256]{1,0:T(8,128)S(1)}, u32[]{:S(2)}, u32[]{:S(2)}) %collective-permute-start) | collective-permute-done | bytes 524320 | tf_op jit(solution)/shard_map/ppermute | solution.py:22
  24.9 0.0 copy-done.6
  24.9 0.6 fusion.2
  25.5 6.9 %collective-permute-done.1 = f32[512,256]{1,0:T(8,128)S(1)} collective-permute-done((f32[512,256]{1,0:T(8,128)S(1)}, f32[512,256]{1,0:T(8,128)S(1)}, u32[]{:S(2)}, u32[]{:S(2)}) %collective-permute-start.1) | collective-permute-done | bytes 524320 | tf_op jit(solution)/shard_map/ppermute | solution.py:22
  32.4 0.2 maximum_multiply_fusion.2
  32.7 1.9 %collective-permute-start.2 = (f32[512,256]{1,0:T(8,128)S(1)}, f32[512,256]{1,0:T(8,128)S(1)}, u32[]{:S(2)}, u32[]{:S(2)}) collective-permute-start(f32[512,256]{1,0:T(8,128)S(1)} %maximum_multiply_fusion.2), channel_id=1, source_target_pairs={{1,0},{2,1},{3,2},{4,3},{5,4},{6,5},{7,6},{8,7},{9,8},{10,9},{11,1... | collective-permute-start | bytes 1572872 | tf_op jit(solution)/shard_map/ppermute | solution.py:22
  34.6 1.0 convolution_bitcast_fusion.3
  35.6 3.4 %collective-permute-start.3 = (f32[512,256]{1,0:T(8,128)S(1)}, f32[512,256]{1,0:T(8,128)S(1)}, u32[]{:S(2)}, u32[]{:S(2)}) collective-permute-start(f32[512,256]{1,0:T(8,128)S(1)} %convolution_bitcast_fusion.3), channel_id=1, source_target_pairs={{0,1},{1,2},{2,3},{3,4},{4,5},{5,6},{6,7},{7,8},{8,9},{9,10},{10,1... | collective-permute-start | bytes 1572872 | tf_op jit(solution)/shard_map/ppermute | solution.py:22
  39.0 0.6 fusion.14
  39.6 6.7 %collective-permute-done.2 = f32[512,256]{1,0:T(8,128)S(1)} collective-permute-done((f32[512,256]{1,0:T(8,128)S(1)}, f32[512,256]{1,0:T(8,128)S(1)}, u32[]{:S(2)}, u32[]{:S(2)}) %collective-permute-start.2) | collective-permute-done | bytes 524320 | tf_op jit(solution)/shard_map/ppermute | solution.py:22
  46.3 0.6 fusion.3
  46.9 5.1 %collective-permute-done.3 = f32[512,256]{1,0:T(8,128)S(1)} collective-permute-done((f32[512,256]{1,0:T(8,128)S(1)}, f32[512,256]{1,0:T(8,128)S(1)}, u32[]{:S(2)}, u32[]{:S(2)}) %collective-permute-start.3) | collective-permute-done | bytes 524320 | tf_op jit(solution)/shard_map/ppermute | solution.py:22
  52.0 0.2 maximum_multiply_fusion.1
  52.2 1.9 %collective-permute-start.4 = (f32[512,256]{1,0:T(8,128)S(1)}, f32[512,256]{1,0:T(8,128)S(1)}, u32[]{:S(2)}, u32[]{:S(2)}) collective-permute-start(f32[512,256]{1,0:T(8,128)S(1)} %maximum_multiply_fusion.1), channel_id=1, source_target_pairs={{1,0},{2,1},{3,2},{4,3},{5,4},{6,5},{7,6},{8,7},{9,8},{10,9},{11,1... | collective-permute-start | bytes 1572872 | tf_op jit(solution)/shard_map/ppermute | solution.py:22
  54.2 1.0 convolution_bitcast_fusion.2
  55.2 3.4 %collective-permute-start.5 = (f32[512,256]{1,0:T(8,128)S(1)}, f32[512,256]{1,0:T(8,128)S(1)}, u32[]{:S(2)}, u32[]{:S(2)}) collective-permute-start(f32[512,256]{1,0:T(8,128)S(1)} %convolution_bitcast_fusion.2), channel_id=1, source_target_pairs={{0,1},{1,2},{2,3},{3,4},{4,5},{5,6},{6,7},{7,8},{8,9},{9,10},{10,1... | collective-permute-start | bytes 1572872 | tf_op jit(solution)/shard_map/ppermute | solution.py:22
  58.5 0.6 fusion.15
  59.1 6.7 %collective-permute-done.4 = f32[512,256]{1,0:T(8,128)S(1)} collective-permute-done((f32[512,256]{1,0:T(8,128)S(1)}, f32[512,256]{1,0:T(8,128)S(1)}, u32[]{:S(2)}, u32[]{:S(2)}) %collective-permute-start.4) | collective-permute-done | bytes 524320 | tf_op jit(solution)/shard_map/ppermute | solution.py:22
  65.9 0.6 fusion.4
  66.5 4.2 %collective-permute-done.5 = f32[512,256]{1,0:T(8,128)S(1)} collective-permute-done((f32[512,256]{1,0:T(8,128)S(1)}, f32[512,256]{1,0:T(8,128)S(1)}, u32[]{:S(2)}, u32[]{:S(2)}) %collective-permute-start.5) | collective-permute-done | bytes 524320 | tf_op jit(solution)/shard_map/ppermute | solution.py:22
  70.7 0.2 maximum_multiply_fusion
  70.9 0.0 copy-start.4
  70.9 0.3 convolution_bitcast_fusion
  71.3 1.9 %collective-permute-start.6 = (f32[512,256]{0,1:T(8,128)S(1)}, f32[512,256]{0,1:T(8,128)S(1)}, u32[]{:S(2)}, u32[]{:S(2)}) collective-permute-start(f32[512,256]{0,1:T(8,128)S(1)} %convolution_bitcast_fusion), channel_id=1, source_target_pairs={{0,8},{8,0},{1,9},{9,1},{2,10},{10,2},{3,11},{11,3},{4,12},{12,4},... | collective-permute-start | bytes 1572872 | tf_op jit(solution)/shard_map/ppermute | solution.py:127
  73.2 1.9 %collective-permute-done.6 = f32[512,256]{0,1:T(8,128)S(1)} collective-permute-done((f32[512,256]{0,1:T(8,128)S(1)}, f32[512,256]{0,1:T(8,128)S(1)}, u32[]{:S(2)}, u32[]{:S(2)}) %collective-permute-start.6) | collective-permute-done | bytes 524320 | tf_op jit(solution)/shard_map/ppermute | solution.py:127
  75.1 0.0 copy-done.4
  75.1 0.4 fusion.5
  75.4 1.0 copy.29
  76.4 0.0 copy-start.2
  76.4 8.2 %all-to-all-start = ((f32[8,64,256]{2,1,0:T(8,128)}), f32[8,64,256]{2,1,0:T(8,128)S(1)}, u32[]{:S(2)}, u32[]{:S(2)}) async-start(f32[8,64,256]{2,1,0:T(8,128)} %bitcast.9), calls=%async_computation | async-start | bytes 1048576 | tf_op jit(solution)/shard_map/all_to_all | solution.py:38
  84.6 0.0 copy-done.2
  84.7 8.2 %all-to-all-done = f32[8,64,256]{2,1,0:T(8,128)S(1)} async-done(((f32[8,64,256]{2,1,0:T(8,128)}), f32[8,64,256]{2,1,0:T(8,128)S(1)}, u32[]{:S(2)}, u32[]{:S(2)}) %all-to-all-start) | async-done | bytes 524320 | tf_op jit(solution)/shard_map/all_to_all | solution.py:38
  92.9 0.2 fusion.8
  93.1 17.4 %all_to_all.10 = f32[32,2,256]{2,1,0:T(2,128)S(1)} all-to-all(f32[32,2,256]{2,1,0:T(2,128)S(1)} %reshape.28), channel_id=1, replica_groups=mesh['yh'=4,'yl'=2,'x'=4,'c'=2,'z'=8] {'yh','z'}, dimensions={0} | all-to-all | bytes 131072 | tf_op jit(solution)/shard_map/all_to_all | solution.py:38
  110.5 0.6 reduce_sum.29
  (4 shorter events, 0.1 us)
Async XLA Ops:
  0.6 12.2 %copy-start = (f32[512,512]{1,0:T(8,128)S(1)}, f32[512,512]{1,0:T(8,128)}, u32[]{:S(2)}) copy-start(f32[512,512]{1,0:T(8,128)} %param.11) | copy-start | bytes 3145732
  0.6 16.4 %copy-start.8 = (f32[16]{0:T(128)S(1)}, f32[16]{0:T(128)}, u32[]{:S(2)}) copy-start(f32[16]{0:T(128)} %param.12) | copy-start | bytes 196
  0.7 16.4 %copy-start.7 = (s32[256]{0:T(256)S(1)}, s32[256]{0:T(256)}, u32[]{:S(2)}) copy-start(s32[256]{0:T(256)} %param.13) | copy-start | bytes 3076
  0.7 16.5 %copy-start.1 = (bf16[1024,512]{1,0:T(8,128)(2,1)S(1)}, bf16[1024,512]{1,0:T(8,128)(2,1)}, u32[]{:S(2)}) copy-start(bf16[1024,512]{1,0:T(8,128)(2,1)} %param.14) | copy-start | bytes 3145732
  0.7 24.2 %collective-permute-start = (f32[512,256]{1,0:T(8,128)}, f32[512,256]{1,0:T(8,128)S(1)}, u32[]{:S(2)}, u32[]{:S(2)}) collective-permute-start(f32[512,256]{1,0:T(8,128)} %param.8), channel_id=1, source_target_pairs={{1,0},{2,1},{3,2},{4,3},{5,4},{6,5},{7,6},{8,7},{9,8},{10,9},{11,1... | collective-permute-start | bytes 1572872 | tf_op jit(solution)/shard_map/ppermute | solution.py:22
  12.9 4.8 %copy-start.5 = (f32[512,256]{1,0:T(8,128)S(1)}, f32[512,256]{1,0:T(8,128)}, u32[]{:S(2)}) copy-start(f32[512,256]{1,0:T(8,128)} %param.8) | copy-start | bytes 1572868
  15.0 2.7 %copy-start.3 = (f32[512,512]{1,0:T(8,128)S(1)}, f32[512,512]{1,0:T(8,128)}, u32[]{:S(2)}) copy-start(f32[512,512]{1,0:T(8,128)} %param.10) | copy-start | bytes 3145732
  15.0 17.4 %collective-permute-start.1 = (f32[512,256]{1,0:T(8,128)S(1)}, f32[512,256]{1,0:T(8,128)S(1)}, u32[]{:S(2)}, u32[]{:S(2)}) collective-permute-start(f32[512,256]{1,0:T(8,128)S(1)} %fusion.13), channel_id=1, source_target_pairs={{0,1},{1,2},{2,3},{3,4},{4,5},{5,6},{6,7},{7,8},{8,9},{9,10},{10,1... | collective-permute-start | bytes 1572872 | tf_op jit(solution)/shard_map/ppermute | solution.py:22
  17.7 7.2 %copy-start.6 = (f32[512,256]{1,0:T(8,128)S(1)}, f32[512,256]{1,0:T(8,128)}, u32[]{:S(2)}) copy-start(f32[512,256]{1,0:T(8,128)} %param.9) | copy-start | bytes 1572868
  32.7 13.7 %collective-permute-start.2 = (f32[512,256]{1,0:T(8,128)S(1)}, f32[512,256]{1,0:T(8,128)S(1)}, u32[]{:S(2)}, u32[]{:S(2)}) collective-permute-start(f32[512,256]{1,0:T(8,128)S(1)} %maximum_multiply_fusion.2), channel_id=1, source_target_pairs={{1,0},{2,1},{3,2},{4,3},{5,4},{6,5},{7,6},{8,7},{9,8},{10,9},{11,1... | collective-permute-start | bytes 1572872 | tf_op jit(solution)/shard_map/ppermute | solution.py:22
  35.6 16.4 %collective-permute-start.3 = (f32[512,256]{1,0:T(8,128)S(1)}, f32[512,256]{1,0:T(8,128)S(1)}, u32[]{:S(2)}, u32[]{:S(2)}) collective-permute-start(f32[512,256]{1,0:T(8,128)S(1)} %convolution_bitcast_fusion.3), channel_id=1, source_target_pairs={{0,1},{1,2},{2,3},{3,4},{4,5},{5,6},{6,7},{7,8},{8,9},{9,10},{10,1... | collective-permute-start | bytes 1572872 | tf_op jit(solution)/shard_map/ppermute | solution.py:22
  52.2 13.7 %collective-permute-start.4 = (f32[512,256]{1,0:T(8,128)S(1)}, f32[512,256]{1,0:T(8,128)S(1)}, u32[]{:S(2)}, u32[]{:S(2)}) collective-permute-start(f32[512,256]{1,0:T(8,128)S(1)} %maximum_multiply_fusion.1), channel_id=1, source_target_pairs={{1,0},{2,1},{3,2},{4,3},{5,4},{6,5},{7,6},{8,7},{9,8},{10,9},{11,1... | collective-permute-start | bytes 1572872 | tf_op jit(solution)/shard_map/ppermute | solution.py:22
  55.2 15.5 %collective-permute-start.5 = (f32[512,256]{1,0:T(8,128)S(1)}, f32[512,256]{1,0:T(8,128)S(1)}, u32[]{:S(2)}, u32[]{:S(2)}) collective-permute-start(f32[512,256]{1,0:T(8,128)S(1)} %convolution_bitcast_fusion.2), channel_id=1, source_target_pairs={{0,1},{1,2},{2,3},{3,4},{4,5},{5,6},{6,7},{7,8},{8,9},{9,10},{10,1... | collective-permute-start | bytes 1572872 | tf_op jit(solution)/shard_map/ppermute | solution.py:22
  70.9 4.2 %copy-start.4 = (f32[512,256]{1,0:T(8,128)}, f32[512,256]{1,0:T(8,128)S(1)}, u32[]{:S(2)}) copy-start(f32[512,256]{1,0:T(8,128)S(1)} %maximum_multiply_fusion) | copy-start | bytes 1572868
  71.3 3.8 %collective-permute-start.6 = (f32[512,256]{0,1:T(8,128)S(1)}, f32[512,256]{0,1:T(8,128)S(1)}, u32[]{:S(2)}, u32[]{:S(2)}) collective-permute-start(f32[512,256]{0,1:T(8,128)S(1)} %convolution_bitcast_fusion), channel_id=1, source_target_pairs={{0,8},{8,0},{1,9},{9,1},{2,10},{10,2},{3,11},{11,3},{4,12},{12,4},... | collective-permute-start | bytes 1572872 | tf_op jit(solution)/shard_map/ppermute | solution.py:127
  76.4 8.2 %copy-start.2 = (f32[256,256]{1,0:T(8,128)S(1)}, f32[256,256]{1,0:T(8,128)}, u32[]{:S(2)}) copy-start(f32[256,256]{1,0:T(8,128)} %block_ref.1) | copy-start | bytes 786436
  76.4 16.4 %all-to-all-start = ((f32[8,64,256]{2,1,0:T(8,128)}), f32[8,64,256]{2,1,0:T(8,128)S(1)}, u32[]{:S(2)}, u32[]{:S(2)}) async-start(f32[8,64,256]{2,1,0:T(8,128)} %bitcast.9), calls=%async_computation | async-start | bytes 1048576 | tf_op jit(solution)/shard_map/all_to_all | solution.py:38
